TPU v7x, 256 devices: a whole 4x4x8 slice. The times are simulated.
256 devices in a mesh: tile: 32 (over y, z), band: 8 (over x, core).
Axes of the slice: x: 4, y: 4, z: 8, core: 2. Of those that a mesh axis runs over, the one named last changes fastest.
Arguments:
- observed: float32 [96, 16384, 128], P('band', 'tile'), may hold values from 0 to 4
- weights: float32 [96, 16384, 128], P('band', 'tile'), may hold values from 0.2 to 6, as said below
- morphology: float32 [4, 16384, 128], P(None, 'tile'), may hold values from 0 to 1
- spectra: float32 [4, 96, 8192], P(None, 'band', 'tile'), may hold values from 0.2 to 2
- blend_blocks: int32 [32, 256], P('tile'), may hold values from 1 to 4, 512 in all within a row
- source_count: int32 [8192], P('tile'), may hold values from 1 to 4
- sent_blocks: int32 [32, 32, 4], P('tile'), may hold values from 0 to 512, as said below
- landing_blocks: int32 [32, 32, 4], P('tile'), may hold values from 0 to 512, as said below
Outputs:
- new_morphology: float32 [4, 16384, 128], P(None, 'tile')
- new_spectra: float32 [4, 96, 8192], P(None, 'band', 'tile')
- misfit: float32 [8192], P('tile')
Inputs may be any that keep to these rules, and one draw needn't show every extreme that they name: `weights`: Positive. `sent_blocks`: entry [s, d, j] is a block of tile index s whose model margins a block of tile index d, or 512 for an empty slot; at most 4 live slots from one sender to one receiver, the live ones first; every sender fills all 4 slots to some receiver and every receiver gets all 4 from some sender; a block may appear in several slots. `landing_blocks`: entry [d, s, j] is the block of tile index d on which slot j from sender s lands, or 512 exactly where sent_blocks[s, d, j] is 512; several slots may land on one block.
All inputs are finite; a program needn't handle non-finite values.
Results may differ from a plain program's by a relative error of at most 0.0003.
Values sent between devices are 32-bit elements; how exact they have to be, the bound alone decides.
No kernel may reach another device: no remote copies, remote signals or barrier semaphores. Data moves between devices by JAX's collectives and lax.ppermute only.
A program may use at most 128 MiB of HBM per device.

v0:
```python
import functools

import jax
import jax.numpy as jnp
from jax import lax
from jax.experimental import pallas as pl
from jax.experimental.pallas import tpu as pltpu
from jax.sharding import PartitionSpec as P


ITERS = 2
F32 = jnp.float32
BF16 = jnp.bfloat16
HIGH = lax.Precision.HIGHEST
KPAD = 16
ROWS = 10
GROUP = 6
SMALL = 8 << 20
EXTRA = 8
NN = (((1,), (0,)), ((), ()))
NT = (((1,), (1,)), ((), ()))
TN = (((0,), (0,)), ((), ()))


def halves(x):
    hi = x.astype(BF16)
    return hi, (x - hi.astype(F32)).astype(BF16)


def pick(onehot, x, dims=NN):
    n = x.shape[1]
    both = jnp.concatenate(halves(x), axis=1)
    y = lax.dot_general(onehot, both, dims, preferred_element_type=F32)
    return y[:, :n] + y[:, n:]


def exact(a, b, dims):
    return lax.dot_general(a, b, dims, precision=HIGH, preferred_element_type=F32)


def iota(shape, dim):
    return lax.broadcasted_iota(jnp.int32, shape, dim)


def hot(mask):
    return jnp.where(mask, 1.0, 0.0).astype(BF16)


def slot_row(idx):
    cap, peers = idx.shape
    slots = cap * peers
    spread = hot(iota((peers, slots), 1) % peers == iota((peers, slots), 0))
    hi, lo = halves(idx.astype(F32))
    wide = jnp.dot(hi, spread, preferred_element_type=F32) + jnp.dot(
        lo, spread, preferred_element_type=F32
    )
    own = iota((cap, slots), 1) // peers == iota((cap, slots), 0)
    return jnp.sum(jnp.where(own, wide, 0.0), axis=0, keepdims=True)


def slot_column(idx):
    row = slot_row(idx)
    n = row.shape[1]
    return jnp.sum(jnp.where(iota((n, n), 0) == iota((n, n), 1), row, 0.0), axis=1, keepdims=True)


def slots_by_block(idx, blocks):
    slots = idx.shape[0] * idx.shape[1]
    return hot(slot_column(idx) == iota((slots, blocks), 1).astype(F32))


def blocks_by_slot(idx, blocks):
    slots = idx.shape[0] * idx.shape[1]
    return hot(slot_row(idx) == iota((blocks, slots), 0).astype(F32))


def membership_of(lengths, blocks, first=0):
    n = lengths.shape[1]
    upto = hot(iota((n, n), 0) <= iota((n, n), 1))
    rows = jnp.broadcast_to(lengths.astype(F32), (8, n))
    ends = lax.dot_general(rows.astype(BF16), upto, NN, preferred_element_type=F32)[:1]
    starts = ends - lengths.astype(F32)
    position = (iota((blocks, n), 0) + first).astype(F32)
    return hot((position >= starts) & (position < ends))


def band_place():
    me = lax.axis_index("band")
    return me // 2, me % 2


def write_message(out, leaving, colours):
    peers = out.shape[0] // ROWS
    lane = iota((peers, 128), 1)
    for k2 in range(2):
        for j in range(4):
            out[pl.ds(k2 * 4 + j, peers, stride=ROWS), :] = leaving[k2][j * peers : (j + 1) * peers]
    for jj in range(2):
        low = colours[jj * peers : (jj + 1) * peers]
        high = colours[(jj + 2) * peers : (jj + 3) * peers]
        out[pl.ds(8 + jj, peers, stride=ROWS), :] = jnp.where(lane < 64, low, high)


def colour_table(member, colour):
    twice = jnp.concatenate([colour, colour], axis=0)
    hi, lo = halves(twice)
    mid = lax.dot_general(member, hi, NT, preferred_element_type=F32)
    return mid + lax.dot_general(member, lo, NT, preferred_element_type=F32)


def started(copies):
    for c in copies:
        c.start()
    return copies


def begin(spectra, lengths, counts, colour, blocks):
    _, h = band_place()
    channels, _, blends = spectra.shape
    member = membership_of(lengths[...], blocks)
    rel = iota((8, blends), 0)
    absolute = jnp.where(rel < 4, rel ^ (2 * h), 8)
    live = jnp.where(absolute < counts[...], 1.0, 0.0).astype(F32)
    colour[...] = jnp.zeros(colour.shape, F32)
    for c in range(channels):
        for k in range(4):
            colour[pl.ds(k * KPAD + c, 1), :] = spectra[c, pl.ds(k ^ (2 * h), 1), :]
    for k in range(4):
        at = pl.ds(k * KPAD, KPAD)
        colour[at, :] = colour[at, :] * live[k : k + 1]
    wide = jnp.concatenate([live, jnp.zeros((120, blends), F32)], axis=0).astype(BF16)
    ab = lax.dot_general(member, wide, NT, preferred_element_type=F32)
    return live, ab, colour_table(member, colour[...])


def first_kernel(
    morph_far,
    spectra_far,
    lengths_far,
    counts_far,
    sent_far,
    message_far,
    morph,
    spectra,
    lengths,
    counts,
    sent,
    colour,
    message,
    sems,
):
    _, h = band_place()
    near = (lengths, counts, spectra, sent, morph)
    far = (lengths_far, counts_far, spectra_far, sent_far, morph_far.at[pl.ds(2 * h, 2)])
    arrivals = started(
        [pltpu.make_async_copy(f, n, sems.at[i]) for i, (f, n) in enumerate(zip(far, near))]
    )
    blocks = morph.shape[1]
    for c in arrivals[:3]:
        c.wait()
    _, ab, table = begin(spectra, lengths, counts, colour, blocks)
    for c in arrivals[3:]:
        c.wait()
    take = slots_by_block(sent[0], blocks)
    leaving = [pick(take, morph[k2] * ab[:, k2 : k2 + 1]) for k2 in range(2)]
    write_message(message, leaving, pick(take, table))
    pltpu.sync_copy(message, message_far)


def start_kernel(
    morph, spectra, lengths, counts, sent, land, own, other, colour, alive, table, ablk, *kept
):
    _, h = band_place()
    live, ab, rows = begin(spectra, lengths, counts, colour, own.shape[1])
    alive[...] = live
    ablk[...] = ab
    table[...] = rows
    for k2 in range(2):
        own[k2] = morph[k2 ^ (2 * h)] * ab[:, k2 : k2 + 1]
        other[k2] = morph[(k2 + 2) ^ (2 * h)] * ab[:, k2 + 2 : k2 + 3]
    for copy, value in zip(kept, (lengths, sent, land)):
        copy[...] = value[...]


def model_kernel(table, own, other, observed_far, out_far, observed, out, sem_in, sem_out):
    channels, blocks, _ = observed.shape

    def there(t):
        return slice(None), pl.ds(pl.multiple_of(t * 128, 128), 128)

    def arrival(t):
        return pltpu.make_async_copy(observed_far.at[there(t)], observed.at[there(t)], sem_in.at[t])

    def leaving(t):
        return pltpu.make_async_copy(out.at[there(t)], out_far.at[there(t)], sem_out.at[t])

    for t in range(blocks // 128):
        arrival(t).start()

    def tile(t, carry):
        arrival(t).wait()
        rows = pl.ds(pl.multiple_of(t * 128, 128), 128)
        cb = table[rows, :]
        sh = [own[0, rows, :], own[1, rows, :], other[0, rows, :], other[1, rows, :]]
        for c in range(channels):
            m = sh[0] * cb[:, c : c + 1]
            for k in range(1, 4):
                m = m + sh[k] * cb[:, k * KPAD + c : k * KPAD + c + 1]
            out[c, rows, :] = m - observed[c, rows, :]
        leaving(t).start()
        return carry

    lax.fori_loop(0, blocks // 128, tile, 0)
    for t in range(blocks // 128):
        leaving(t).wait()


def link_kernel(
    last,
    mine,
    partner,
    resid_far,
    weights_far,
    land,
    wout_far,
    keep,
    send,
    miss,
    shs,
    back,
    sbs,
    ssb,
    macc,
    resid,
    weights,
    wout,
    sem_r,
    sem_w,
    sem_out,
):
    channels, blocks, pixels = resid.shape
    peers = land.shape[2]
    slots = 4 * peers

    def arrivals(c):
        return (
            pltpu.make_async_copy(resid_far.at[c], resid.at[c], sem_r.at[c]),
            pltpu.make_async_copy(weights_far.at[c], weights.at[c], sem_w.at[c]),
        )

    def gone(c):
        return pltpu.make_async_copy(wout.at[c], wout_far.at[c], sem_out.at[c])

    for c in range(GROUP):
        started(arrivals(c))
    sbs[...] = blocks_by_slot(land[0], blocks)
    ssb[...] = slots_by_block(land[0], blocks)
    for k2 in range(2):
        for j in range(4):
            rows = pl.ds(j * peers, peers)
            shs[k2, rows, :] = mine[pl.ds(k2 * 4 + j, peers, stride=ROWS), :]
            shs[k2 + 2, rows, :] = partner[pl.ds(k2 * 4 + j, peers, stride=ROWS), :]
    back[...] = jnp.zeros(back.shape, F32)
    if last:
        macc[...] = jnp.zeros(macc.shape, F32)
    lane = iota((peers, 128), 1)

    def group(g, carry):
        ci, bc = carry[:2], list(carry[2:])

        @pl.when(g + 1 < channels // GROUP)
        def _():
            for u in range(GROUP):
                started(arrivals((g + 1) * GROUP + u))

        for u in range(GROUP):
            for a in arrivals(g * GROUP + u):
                a.wait()
        for u in range(GROUP):
            c = g * GROUP + u
            parts = []
            for j in range(4):
                rows = pl.ds(j * peers, peers)
                at = u + (64 if j >= 2 else 0)
                m = shs[0, rows, :] * ci[j % 2][:, at : at + 1]
                for k in range(1, 4):
                    col = at + k * KPAD
                    m = m + shs[k, rows, :] * ci[j % 2][:, col : col + 1]
                parts.append(m)
            both = jnp.concatenate(halves(jnp.concatenate(parts, axis=0)), axis=1)
            landed = jnp.zeros((slots, 2 * pixels), F32)
            for q in range(blocks // 128):
                rows = pl.ds(q * 128, 128)
                y = jnp.dot(sbs[rows, :], both, preferred_element_type=F32)
                x = resid[c, rows, :] + (y[:, :pixels] + y[:, pixels:])
                wt = weights[c, rows, :] * x
                wout[c, rows, :] = wt
                if last:
                    macc[rows, :] += wt * x
                wboth = jnp.concatenate(halves(wt), axis=1)
                landed = landed + jnp.dot(ssb[:, rows], wboth, preferred_element_type=F32)
            landed = landed[:, :pixels] + landed[:, pixels:]
            for j in range(4):
                rows = pl.ds(j * peers, peers)
                at = u + (64 if j >= 2 else 0)
                ld = landed[j * peers : (j + 1) * peers]
                for k in range(4):
                    col = at + k * KPAD
                    back[k, rows, :] += ci[j % 2][:, col : col + 1] * ld
                    r = jnp.sum(shs[k, rows, :] * ld, axis=1, keepdims=True)
                    bc[j % 2] = jnp.where(lane == col, r, bc[j % 2])
        for u in range(GROUP):
            gone(g * GROUP + u).start()
        return tuple(pltpu.roll(v, 128 - GROUP, 1) for v in (*ci, *bc))

    ci = tuple(mine[pl.ds(8 + jj, peers, stride=ROWS), :] for jj in range(2))
    none = jnp.zeros((peers, 128), F32)
    done = lax.fori_loop(0, channels // GROUP, group, (*ci, none, none))
    bc = [pltpu.roll(v, channels, 1) for v in done[2:]]
    keep[...] = jnp.zeros(keep.shape, F32)
    send[...] = jnp.zeros(send.shape, F32)
    for k2 in range(2):
        for j in range(4):
            rows = pl.ds(j * peers, peers)
            keep[pl.ds(k2 * 4 + j, peers, stride=ROWS), :] = back[k2, rows, :]
            send[pl.ds(k2 * 4 + j, peers, stride=ROWS), :] = back[k2 + 2, rows, :]
    for jj in range(2):
        keep[pl.ds(8 + jj, peers, stride=ROWS), :] = bc[jj]
    if last:
        miss[...] = exact(jnp.ones((8, pixels), F32), macc[...], NT)
    else:
        miss[...] = jnp.zeros(miss.shape, F32)
    for c in range(channels):
        gone(c).wait()


def grad_kernel(
    table, own, other, wgt_far, colour, lengths, miss, after, keep, send, per_block, wgt, sems
):
    channels, blocks, _ = wgt.shape

    def arrival(t):
        there = slice(None), pl.ds(pl.multiple_of(t * 128, 128), 128)
        return pltpu.make_async_copy(wgt_far.at[there], wgt.at[there], sems.at[t])

    for t in range(blocks // 128):
        arrival(t).start()
    lane = iota((128, 128), 1)
    quarter = blocks // 4

    def colours(t, carry):
        arrival(t).wait()
        rows = pl.ds(pl.multiple_of(t * 128, 128), 128)
        sh = [own[0, rows, :], own[1, rows, :], other[0, rows, :], other[1, rows, :]]
        pb = jnp.zeros((128, 128), F32)
        for c in range(channels):
            wt = wgt[c, rows, :]
            for k in range(4):
                r = jnp.sum(sh[k] * wt, axis=1, keepdims=True)
                pb = jnp.where(lane == k * KPAD + c, r, pb)
        per_block[rows, :] = pb
        return carry

    lax.fori_loop(0, blocks // 128, colours, 0)

    def shapes(t, carry):
        q, inside = t // 2, pl.multiple_of((t % 2) * 64, 64)
        rows = pl.ds(pl.multiple_of(t * 64, 64), 64)
        cb = table[rows, :]
        gs = [None] * 4
        for c in range(channels):
            wt = wgt[c, rows, :]
            for k in range(4):
                term = cb[:, k * KPAD + c : k * KPAD + c + 1] * wt
                gs[k] = term if c == 0 else gs[k] + term
        for k2 in range(2):
            keep[q, pl.ds(k2 * quarter + inside, 64), :] = gs[k2]
            send[q, pl.ds(k2 * quarter + inside, 64), :] = gs[k2 + 2]
        return carry

    lax.fori_loop(0, blocks // 64, shapes, 0)
    member = membership_of(lengths[...], blocks)
    sq = colour[...] * colour[...]
    rows8 = iota((8, sq.shape[1]), 0)
    power = jnp.zeros((8, sq.shape[1]), F32)
    for k in range(4):
        total = jnp.sum(sq[k * KPAD : (k + 1) * KPAD], axis=0, keepdims=True)
        power = jnp.where(rows8 == k, total, power)
    hi, lo = halves(power)
    wide = lax.dot_general(hi, member, NT, preferred_element_type=F32) + lax.dot_general(
        lo, member, NT, preferred_element_type=F32
    )
    for q in range(4):
        w = wide[:, q * quarter : (q + 1) * quarter]
        m = miss[0:1, q * quarter : (q + 1) * quarter]
        r = iota((8, quarter), 0)
        first = jnp.where(r == 0, m, jnp.where(r == 1, w[0:1], jnp.where(r == 2, w[1:2], 0.0)))
        second = jnp.where(r == 0, m, jnp.where(r == 1, w[2:3], jnp.where(r == 2, w[3:4], 0.0)))
        keep[q, pl.ds(2 * quarter, EXTRA), :] = first
        send[q, pl.ds(2 * quarter, EXTRA), :] = second


def merge_kernel(arrived, keep, came, sent, p0, p1, p2, p3, scat):
    x, _ = band_place()
    peers = sent.shape[2]
    quarter = (p0.shape[0] - EXTRA) // 2
    blocks = 4 * quarter
    put = blocks_by_slot(sent[0], blocks)
    for k2 in range(2):
        rows = [arrived[pl.ds(k2 * 4 + j, peers, stride=ROWS), :] for j in range(4)]
        scat[k2] = pick(put, jnp.concatenate(rows, axis=0))
    for step, out in enumerate((p0, p1, p2, p3)):
        q = lax.rem(x + step, 4)
        out[...] = keep[q] + came[q]
        for k2 in range(2):
            at = pl.ds(pl.multiple_of(q * quarter, quarter), quarter)
            out[pl.ds(k2 * quarter, quarter), :] += scat[k2, at, :]


def colour_kernel(
    last, arrived, sent, per_block, lengths, own, other, colour, alive, *outs
):
    if last:
        out, fresh = outs
    else:
        fresh, table = outs
    blocks = per_block.shape[0]
    peers = sent.shape[2]
    member = membership_of(lengths[...], blocks)
    put = blocks_by_slot(sent[0], blocks)
    lane = iota((peers, 128), 1)
    rows = []
    for j in range(4):
        row = arrived[pl.ds(8 + j % 2, peers, stride=ROWS), :]
        rows.append(jnp.where((lane < 64) == (j < 2), row, 0.0))
    total = per_block[...] + pick(put, jnp.concatenate(rows, axis=0))
    hi, lo = halves(total)
    grad = lax.dot_general(hi, member, TN, preferred_element_type=F32) + lax.dot_general(
        lo, member, TN, preferred_element_type=F32
    )
    grad = grad[:64] + grad[64:]
    ones = jnp.ones((8, own.shape[2]), F32)
    for k in range(4):
        s = own[k] if k < 2 else other[k - 2]
        by_block = exact(ones, s * s, NT)
        hi, lo = halves(by_block)
        power = lax.dot_general(hi, member, NN, preferred_element_type=F32) + lax.dot_general(
            lo, member, NN, preferred_element_type=F32
        )
        step = 1.0 / (1.0 + power[:1])
        at = pl.ds(k * KPAD, KPAD)
        new = (
            jnp.maximum(colour[at, :] - step * grad[k * KPAD : (k + 1) * KPAD], 0.0)
            * alive[k : k + 1, :]
        )
        fresh[at, :] = new
    if last:
        _, h = band_place()
        for c in range(out.shape[0]):
            for k in range(4):
                out[c, pl.ds(k ^ (2 * h), 1), :] = fresh[pl.ds(k * KPAD + c, 1), :]
    else:
        table[...] = colour_table(member, fresh[...])


def update_kernel(p0, r1, r2, r3, own, ablk, out):
    x, _ = band_place()
    quarter = (p0.shape[0] - EXTRA) // 2
    total = p0[...] + r1[...] + r2[...] + r3[...]
    at = pl.ds(pl.multiple_of(x * quarter, quarter), quarter)
    ab = ablk[at, :]
    eye = iota((quarter, quarter), 0) == iota((quarter, quarter), 1)
    for k2 in range(2):
        row = total[2 * quarter + 1 + k2 : 2 * quarter + 2 + k2]
        power = jnp.sum(jnp.where(eye, row, 0.0), axis=1, keepdims=True)
        step = 1.0 / (1.0 + power)
        g = total[k2 * quarter : (k2 + 1) * quarter]
        out[pl.ds(k2 * quarter, quarter), :] = (
            jnp.maximum(own[k2, at, :] - step * g, 0.0) * ab[:, k2 : k2 + 1]
        )
    out[pl.ds(2 * quarter, EXTRA), :] = total[2 * quarter :]


def leave_kernel(n0, r1, r2, r3, table, sent, pair, message_far, message):
    x, _ = band_place()
    quarter = (n0.shape[0] - EXTRA) // 2
    for step, piece in enumerate((n0, r1, r2, r3)):
        q = lax.rem(x + 4 - step, 4)
        at = pl.ds(pl.multiple_of(q * quarter, quarter), quarter)
        for k2 in range(2):
            pair[k2, at, :] = piece[pl.ds(k2 * quarter, quarter), :]
    take = slots_by_block(sent[0], 4 * quarter)
    write_message(message, [pick(take, pair[0]), pick(take, pair[1])], pick(take, table[...]))
    pltpu.sync_copy(message, message_far)


def finish_kernel(n0, r1, r2, r3, m0, m1, m2, m3, lengths, shape, misfit):
    x, h = band_place()
    quarter = (n0.shape[0] - EXTRA) // 2
    total = jnp.zeros((8, lengths.shape[1]), F32)
    for step, (mine, theirs) in enumerate(((n0, m0), (r1, m1), (r2, m2), (r3, m3))):
        q = lax.rem(x + 4 - step, 4)
        at = pl.ds(pl.multiple_of(q * quarter, quarter), quarter)
        for k2 in range(2):
            shape[k2 + 2 * h, at, :] = mine[pl.ds(k2 * quarter, quarter), :]
            shape[k2 + 2 * (1 - h), at, :] = theirs[pl.ds(k2 * quarter, quarter), :]
        ms = mine[pl.ds(2 * quarter, EXTRA), :]
        part = membership_of(lengths[...], quarter, q * quarter)
        hi, lo = halves(ms)
        total = total + lax.dot_general(hi, part, NN, preferred_element_type=F32)
        total = total + lax.dot_general(lo, part, NN, preferred_element_type=F32)
    misfit[...] = total[:1]


def call(kernel, outs, args, scratch=(), limit=54_000_000, cost=3e6, far_in=(), far_out=()):
    many = isinstance(outs, list)
    shapes = [
        s if isinstance(s, jax.ShapeDtypeStruct) else jax.ShapeDtypeStruct(s, F32)
        for s in (outs if many else [outs])
    ]
    near = pl.BlockSpec(memory_space=pltpu.VMEM)
    far = pl.BlockSpec(memory_space=pltpu.HBM)
    got = pl.pallas_call(
        kernel,
        out_shape=shapes,
        in_specs=[far if i in far_in else near for i in range(len(args))],
        out_specs=[far if i in far_out else near for i in range(len(shapes))],
        scratch_shapes=list(scratch),
        compiler_params=pltpu.CompilerParams(vmem_limit_bytes=limit),
        cost_estimate=pl.CostEstimate(flops=0, bytes_accessed=int(cost), transcendentals=0),
    )(*args)
    return got if many else got[0]


def on_device(
    observed, weights, morphology, spectra, blend_blocks, source_count, sent_blocks, landing_blocks
):
    channels, blocks, pixels = observed.shape
    spectra = spectra.transpose(1, 0, 2)
    sent_blocks = sent_blocks.transpose(0, 2, 1)
    landing_blocks = landing_blocks.transpose(0, 2, 1)
    blends = spectra.shape[2]
    peers = sent_blocks.shape[2]
    slots = 4 * peers
    quarter = blocks // 4
    piece = (2 * quarter + EXTRA, pixels)
    pair = (2, blocks, pixels)
    message = (peers * ROWS, pixels)
    band = lax.axis_size("band")

    def over_core(v):
        return lax.ppermute(v, "band", [(i, i ^ 1) for i in range(band)])

    def over_x(v, step):
        return lax.ppermute(v, "band", [(i, (i + 2 * step) % band) for i in range(band)])

    def over_tile(v):
        v = v.reshape(peers, ROWS // 2, 2, pixels)
        return lax.all_to_all(v, "tile", 0, 0, tiled=True).reshape(message)

    counts = source_count.reshape(1, blends)
    colour_rows = (4 * KPAD, blends)
    table_rows = (blocks, 128)

    def kept(v):
        return jax.ShapeDtypeStruct(v.shape, v.dtype)

    def dma(n):
        return pltpu.SemaphoreType.DMA((n,))

    cube = pltpu.VMEM(observed.shape, F32)
    leaving = call(
        first_kernel,
        message,
        (morphology, spectra, blend_blocks, counts, sent_blocks),
        scratch=(
            pltpu.VMEM(pair, F32),
            pltpu.VMEM(spectra.shape, F32),
            pltpu.VMEM(blend_blocks.shape, jnp.int32),
            pltpu.VMEM(counts.shape, jnp.int32),
            pltpu.VMEM(sent_blocks.shape, jnp.int32),
            pltpu.VMEM(colour_rows, F32),
            pltpu.VMEM(message, F32),
            dma(5),
        ),
        limit=67_043_328,
        far_in=range(5),
        far_out=(0,),
    )
    own, other, colour, alive, table, ablk, lengths, sent, land = call(
        start_kernel,
        [
            pair,
            pair,
            colour_rows,
            (8, blends),
            table_rows,
            table_rows,
            kept(blend_blocks),
            kept(sent_blocks),
            kept(landing_blocks),
        ],
        (morphology, spectra, blend_blocks, counts, sent_blocks, landing_blocks),
    )
    for iteration in range(ITERS):
        last = iteration == ITERS - 1
        mine = over_tile(leaving)
        resid = call(
            model_kernel,
            observed.shape,
            (table, own, other, observed),
            scratch=(cube, cube, dma(blocks // 128), dma(blocks // 128)),
            cost=16e6,
            far_in=(3,),
            far_out=(0,),
        )
        mine, resid = lax.optimization_barrier((mine, resid))
        partner = over_core(mine)
        wgt, bkeep, bsend, miss = call(
            functools.partial(link_kernel, last),
            [observed.shape, message, message, (8, blocks)],
            (mine, partner, resid, weights, land),
            scratch=(
                pltpu.VMEM((4, slots, pixels), F32),
                pltpu.VMEM((4, slots, pixels), F32),
                pltpu.VMEM((blocks, slots), BF16),
                pltpu.VMEM((slots, blocks), BF16),
                pltpu.VMEM((blocks, pixels), F32),
                cube,
                cube,
                cube,
                dma(channels),
                dma(channels),
                dma(channels),
            ),
            cost=14e6,
            far_in=(2, 3),
            far_out=(0,),
        )
        returning = bkeep + over_core(bsend)
        back = over_tile(returning)
        gkeep, gsend, per_block = call(
            grad_kernel,
            [(4,) + piece, (4,) + piece, table_rows],
            (table, own, other, wgt, colour, lengths, miss, returning),
            scratch=(cube, dma(blocks // 128)),
            cost=30e6,
            far_in=(3, 7),
        )
        gcame = over_core(gsend)
        p0, p1, p2, p3 = call(
            merge_kernel,
            [piece] * 4,
            (back, gkeep, gcame, sent),
            scratch=(pltpu.VMEM(pair, F32),),
            limit=SMALL,
        )
        r1, r2, r3 = (over_x(v, s) for s, v in ((1, p1), (2, p2), (3, p3)))
        colour_args = (back, sent, per_block, lengths, own, other, colour, alive)
        if last:
            new_colour = call(
                functools.partial(colour_kernel, True),
                (channels, 4, blends),
                colour_args,
                scratch=(pltpu.VMEM(colour_rows, F32),),
                limit=SMALL,
                cost=8e6,
            )
        else:
            colour, table = call(
                functools.partial(colour_kernel, False),
                [colour_rows, table_rows],
                colour_args,
                limit=SMALL,
                cost=8e6,
            )
        n0 = call(update_kernel, piece, (p0, r1, r2, r3, own, ablk), limit=SMALL)
        n1, n2, n3 = (over_x(n0, s) for s in (1, 2, 3))
        if not last:
            own, leaving = call(
                leave_kernel, [pair, message], (n0, n1, n2, n3, table, sent),
                scratch=(pltpu.VMEM(message, F32),),
                limit=SMALL,
                far_out=(1,),
            )
            other = over_core(own)
    m0, m1, m2, m3 = (over_core(v) for v in (n0, n1, n2, n3))
    shape, misfit = call(
        finish_kernel,
        [morphology.shape, (1, blends)],
        (n0, n1, n2, n3, m0, m1, m2, m3, lengths),
        limit=SMALL,
    )
    return shape, new_colour.transpose(1, 0, 2), misfit.reshape(blends)


def solution(mesh):
    return jax.shard_map(
        on_device,
        mesh=mesh,
        in_specs=(
            P("band", "tile", None),
            P("band", "tile", None),
            P(None, "tile", None),
            P(None, "band", "tile"),
            P("tile", None),
            P("tile"),
            P("tile", None, None),
            P("tile", None, None),
        ),
        out_specs=(P(None, "tile", None), P(None, "band", "tile"), P("tile")),
        check_vma=False,
    )
```

profile of v0, /device:TPU:1, one launch (start us, length us, event | category | flops | bytes accessed | tf_op | source)
XLA Modules:
  0.0 166.3 jit_solution(6835208181131722400)
XLA Ops:
  0.6 2.7 %shard_map.103 = f32[320,128]{1,0:T(8,128)} custom-call(f32[4,512,128]{2,1,0:T(8,128)} %morph.1, f32[12,4,256]{2,1,0:T(4,128)} %bitcast.24, s32[1,256]{1,0:T(1,128)} %lengths.1, s32[1,256]{1,0:T(1,128)} %bitcast.28, s32[1,4,32]{2,1,0:T(4,128)} %bitcast.26), custom_call_target="tpu_custom_call" | custom-call | bytes 3000000 | tf_op jit(solution)/shard_map/pallas_call | solution.py:523
  3.4 12.0 %all-to-all-start = ((f32[32,5,2,128]{3,2,1,0:T(2,128)}), f32[32,5,2,128]{3,2,1,0:T(2,128)S(1)}, u32[]{:S(2)}, u32[]{:S(2)}) async-start(f32[32,5,2,128]{3,2,1,0:T(2,128)} %bitcast.31), calls=%async_computation | async-start | bytes 327680 | tf_op jit(solution)/shard_map/all_to_all | solution.py:559
  15.4 0.8 copy-done
  16.2 0.7 copy-done.1
  16.9 0.7 copy-done.2
  17.6 0.7 copy-done.3
  18.3 0.7 copy-done.4
  18.9 1.9 %shard_map.104 = (f32[2,512,128]{2,1,0:T(8,128)S(1)}, f32[2,512,128]{2,1,0:T(8,128)S(1)}, f32[64,256]{1,0:T(8,128)S(1)}, f32[8,256]{1,0:T(8,128)S(1)}, f32[512,1...) custom-call(f32[4,512,128]{2,1,0:T(8,128)} %morph.1, ...), custom_call_target="tpu_custom_call" | custom-call | bytes 3000000 | tf_op jit(solution)/shard_map/pallas_call | solution.py:523
  20.9 5.9 %shard_map.105.resid_far = f32[12,512,128]{2,1,0:T(8,128)} custom-call(f32[512,128]{1,0:T(8,128)S(1)} %get-tuple-element.44.table, f32[2,512,128]{2,1,0:T(8,128)S(1)} %get-tuple-element.45.own, f32[2,512,128]{2,1,0:T(8,128)S(1)} %get-tuple-element.46.other, f32[12,512,128]{2,1,0:T(8,128)} %observed_far.3), custom_call_target="tpu_custom_call" | custom-call | bytes 16000000 | tf_op jit(solution)/shard_map/pallas_call | solution.py:523
  26.8 1.0 collective-permute-start
  27.9 1.0 collective-permute-done.partner
  28.9 6.1 %shard_map.106 = (f32[12,512,128]{2,1,0:T(8,128)}, f32[320,128]{1,0:T(8,128)S(1)}, f32[320,128]{1,0:T(8,128)S(1)}, f32[8,512]{1,0:T(8,128)S(1)}) custom-call(f32[320,128]{1,0:T(8,128)S(1)} %bitcast.21, f32[320,128]{1,0:T(8,128)S(1)} %collective-permute-done.partner, f32[12,512,128]{2,1,0:T(8,128)} %shard_map.105.resid_far, f32[12,512,128]{2,1,0:T(8,128)} %weights_far.3, ...), custom_call_target="tpu_custom_call" | custom-call | bytes 14000000 | tf_op jit(solution)/shard_map/pallas_call | solution.py:523
  35.5 1.0 collective-permute-done.1
  36.5 10.3 %shard_map.107 = (f32[4,264,128]{2,1,0:T(8,128)S(1)}, f32[4,264,128]{2,1,0:T(8,128)}, f32[512,128]{1,0:T(8,128)S(1)}) custom-call(f32[512,128]{1,0:T(8,128)S(1)} %get-tuple-element.44.table, f32[2,512,128]{2,1,0:T(8,128)S(1)} %get-tuple-element.45.own, f32[2,512,128]{2,1,0:T(8,128)S(1)} %get-tuple-element.46.other, ...), custom_call_target="tpu_custom_call" | custom-call | bytes 30000000 | tf_op jit(solution)/shard_map/pallas_call | solution.py:523
  47.3 18.6 %all_to_all.20 = f32[32,5,2,128]{3,2,1,0:T(2,128)S(1)} all-to-all(f32[32,5,2,128]{3,2,1,0:T(2,128)S(1)} %bitcast.15), channel_id=1, replica_groups=mesh['tile'=32,'band'=8] {'tile'}, dimensions={0} | all-to-all | bytes 327680 | tf_op jit(solution)/shard_map/all_to_all | solution.py:559
  65.8 0.5 shard_map.108
  66.3 1.3 collective-permute-start.3
  67.6 2.4 %collective-permute-start.4 = (f32[264,128]{1,0:T(8,128)S(1)}, f32[264,128]{1,0:T(8,128)S(1)}, u32[]{:S(2)}, u32[]{:S(2)}) collective-permute-start(f32[264,128]{1,0:T(8,128)S(1)} %get-tuple-element.61), channel_id=1, source_target_pairs={{0,4},{1,5},{2,6},{3,7},{4,0},{5,1},{6,2},{7,3},{8,12},{9,13},{10,... | collective-permute-start | bytes 405512 | tf_op jit(solution)/shard_map/ppermute | solution.py:555
  70.1 1.2 collective-permute-start.5
  71.5 2.5 %collective-permute-done.4.r2 = f32[264,128]{1,0:T(8,128)S(1)} collective-permute-done((f32[264,128]{1,0:T(8,128)S(1)}, f32[264,128]{1,0:T(8,128)S(1)}, u32[]{:S(2)}, u32[]{:S(2)}) %collective-permute-start.4) | collective-permute-done | bytes 135200 | tf_op jit(solution)/shard_map/ppermute | solution.py:555
  74.4 2.2 %collective-permute-start.8 = (f32[264,128]{1,0:T(8,128)S(1)}, f32[264,128]{1,0:T(8,128)S(1)}, u32[]{:S(2)}, u32[]{:S(2)}) collective-permute-start(f32[264,128]{1,0:T(8,128)S(1)} %shard_map.109.n0), channel_id=1, source_target_pairs={{0,6},{1,7},{2,0},{3,1},{4,2},{5,3},{6,4},{7,5},{8,14},{9,15},{10,... | collective-permute-start | bytes 405512 | tf_op jit(solution)/shard_map/ppermute | solution.py:555
  76.6 0.8 collective-permute-start.7
  77.7 2.4 %shard_map.110 = (f32[64,256]{1,0:T(8,128)S(1)}, f32[512,128]{1,0:T(8,128)S(1)}) custom-call(f32[320,128]{1,0:T(8,128)S(1)} %bitcast.19, s32[1,4,32]{2,1,0:T(4,128)S(1)} %get-tuple-element.58.sent, f32[512,128]{1,0:T(8,128)S(1)} %get-tuple-element.64.per_block, s32[1,256]{1,0:T(1,128)S(1)} %get-tuple-element.54.lengths, ...), custom_call_target="tpu_custom_call" | custom-call | bytes 8000000 | tf_op jit(solution)/shard_map/pallas_call | solution.py:523
  80.1 1.9 %collective-permute-done.7.r2 = f32[264,128]{1,0:T(8,128)S(1)} collective-permute-done((f32[264,128]{1,0:T(8,128)S(1)}, f32[264,128]{1,0:T(8,128)S(1)}, u32[]{:S(2)}, u32[]{:S(2)}) %collective-permute-start.7) | collective-permute-done | bytes 135200 | tf_op jit(solution)/shard_map/ppermute | solution.py:555
  82.1 1.3 collective-permute-done.6.r1
  83.4 1.1 shard_map.111
  84.5 5.7 %collective-permute-start.9 = (f32[2,512,128]{2,1,0:T(8,128)S(1)}, f32[2,512,128]{2,1,0:T(8,128)S(1)}, u32[]{:S(2)}, u32[]{:S(2)}) collective-permute-start(f32[2,512,128]{2,1,0:T(8,128)S(1)} %get-tuple-element.68.own), channel_id=1, source_target_pairs={{0,1},{1,0},{2,3},{3,2},{4,5},{5,4},{6,7},{7,6},{8,9},{9,8},{10,11... | collective-permute-start | bytes 1572872 | tf_op jit(solution)/shard_map/ppermute | solution.py:552
  90.3 5.0 %all-to-all-start.2 = ((f32[32,5,2,128]{3,2,1,0:T(2,128)}), f32[32,5,2,128]{3,2,1,0:T(2,128)S(1)}, u32[]{:S(2)}, u32[]{:S(2)}) async-start(f32[32,5,2,128]{3,2,1,0:T(2,128)} %bitcast.8), calls=%async_computation.2 | async-start | bytes 327680 | tf_op jit(solution)/shard_map/all_to_all | solution.py:559
  95.3 5.9 %shard_map.112.resid_far = f32[12,512,128]{2,1,0:T(8,128)} custom-call(f32[512,128]{1,0:T(8,128)S(1)} %get-tuple-element.66.table, f32[2,512,128]{2,1,0:T(8,128)S(1)} %get-tuple-element.68.own, f32[2,512,128]{2,1,0:T(8,128)S(1)} %collective-permute-done.9.other, f32[12,512,128]{2,1,0:T(8,128)} %observed_far.3), custom_call_target="tpu_custom_call" | custom-call | bytes 16000000 | tf_op jit(solution)/shard_map/pallas_call | solution.py:523
  101.2 3.3 %all-to-all-done.2 = f32[32,5,2,128]{3,2,1,0:T(2,128)S(1)} async-done(((f32[32,5,2,128]{3,2,1,0:T(2,128)}), f32[32,5,2,128]{3,2,1,0:T(2,128)S(1)}, u32[]{:S(2)}, u32[]{:S(2)}) %all-to-all-start.2) | async-done | bytes 163872 | tf_op jit(solution)/shard_map/all_to_all | solution.py:559
  104.5 2.6 %collective-permute-start.10 = (f32[320,128]{1,0:T(8,128)S(1)}, f32[320,128]{1,0:T(8,128)S(1)}, u32[]{:S(2)}, u32[]{:S(2)}) collective-permute-start(f32[320,128]{1,0:T(8,128)S(1)} %bitcast.22), channel_id=1, source_target_pairs={{0,1},{1,0},{2,3},{3,2},{4,5},{5,4},{6,7},{7,6},{8,9},{9,8},{10,11... | collective-permute-start | bytes 491528 | tf_op jit(solution)/shard_map/ppermute | solution.py:552
  107.1 1.0 collective-permute-done.10.partner
  108.2 6.1 %shard_map.113 = (f32[12,512,128]{2,1,0:T(8,128)}, f32[320,128]{1,0:T(8,128)S(1)}, f32[320,128]{1,0:T(8,128)S(1)}, f32[8,512]{1,0:T(8,128)S(1)}) custom-call(f32[320,128]{1,0:T(8,128)S(1)} %bitcast.23, f32[320,128]{1,0:T(8,128)S(1)} %collective-permute-done.10.partner, f32[12,512,128]{2,1,0:T(8,128)} %shard_map.112.resid_far, f32[12,512,128]{2,1,0:T(8,128)} %weights_far.3, ...), custom_call_target="tpu_custom_call" | custom-call | bytes 14000000 | tf_op jit(solution)/shard_map/pallas_call | solution.py:523
  114.8 1.0 collective-permute-done.11
  115.8 10.3 %shard_map.114 = (f32[4,264,128]{2,1,0:T(8,128)S(1)}, f32[4,264,128]{2,1,0:T(8,128)}, f32[512,128]{1,0:T(8,128)S(1)}) custom-call(f32[512,128]{1,0:T(8,128)S(1)} %get-tuple-element.66.table, f32[2,512,128]{2,1,0:T(8,128)S(1)} %get-tuple-element.68.own, f32[2,512,128]{2,1,0:T(8,128)S(1)} %collective-permute-done.9.other, ...), custom_call_target="tpu_custom_call" | custom-call | bytes 30000000 | tf_op jit(solution)/shard_map/pallas_call | solution.py:523
  126.6 13.0 %all_to_all.21 = f32[32,5,2,128]{3,2,1,0:T(2,128)S(1)} all-to-all(f32[32,5,2,128]{3,2,1,0:T(2,128)S(1)} %bitcast.14), channel_id=1, replica_groups=mesh['tile'=32,'band'=8] {'tile'}, dimensions={0} | all-to-all | bytes 327680 | tf_op jit(solution)/shard_map/all_to_all | solution.py:559
  140.2 1.5 collective-permute-start.14
  141.6 1.2 collective-permute-start.15
  142.9 3.8 %collective-permute-done.13.r1 = f32[264,128]{1,0:T(8,128)S(1)} collective-permute-done((f32[264,128]{1,0:T(8,128)S(1)}, f32[264,128]{1,0:T(8,128)S(1)}, u32[]{:S(2)}, u32[]{:S(2)}) %collective-permute-start.13) | collective-permute-done | bytes 135200 | tf_op jit(solution)/shard_map/ppermute | solution.py:555
  146.7 0.9 collective-permute-done.15.r3
  147.8 2.1 %collective-permute-start.18 = (f32[264,128]{1,0:T(8,128)S(1)}, f32[264,128]{1,0:T(8,128)S(1)}, u32[]{:S(2)}, u32[]{:S(2)}) collective-permute-start(f32[264,128]{1,0:T(8,128)S(1)} %shard_map.116.n0), channel_id=1, source_target_pairs={{0,6},{1,7},{2,0},{3,1},{4,2},{5,3},{6,4},{7,5},{8,14},{9,15},{10,... | collective-permute-start | bytes 405512 | tf_op jit(solution)/shard_map/ppermute | solution.py:555
  149.9 0.7 collective-permute-start.16
  150.6 4.6 %collective-permute-start.19 = (f32[264,128]{1,0:T(8,128)S(1)}, f32[264,128]{1,0:T(8,128)S(1)}, u32[]{:S(2)}, u32[]{:S(2)}) collective-permute-start(f32[264,128]{1,0:T(8,128)S(1)} %shard_map.116.n0), channel_id=1, source_target_pairs={{0,1},{1,0},{2,3},{3,2},{4,5},{5,4},{6,7},{7,6},{8,9},{9,8},{10,11... | collective-permute-start | bytes 405512 | tf_op jit(solution)/shard_map/ppermute | solution.py:552
  155.2 3.0 %collective-permute-start.22 = (f32[264,128]{1,0:T(8,128)S(1)}, f32[264,128]{1,0:T(8,128)S(1)}, u32[]{:S(2)}, u32[]{:S(2)}) collective-permute-start(f32[264,128]{1,0:T(8,128)S(1)} %collective-permute-done.18.r3), channel_id=1, source_target_pairs={{0,1},{1,0},{2,3},{3,2},{4,5},{5,4},{6,7},{7,6},{8,9},{9,8},{10,11... | collective-permute-start | bytes 405512 | tf_op jit(solution)/shard_map/ppermute | solution.py:552
  158.3 2.6 %collective-permute-start.21 = (f32[264,128]{1,0:T(8,128)S(1)}, f32[264,128]{1,0:T(8,128)S(1)}, u32[]{:S(2)}, u32[]{:S(2)}) collective-permute-start(f32[264,128]{1,0:T(8,128)S(1)} %collective-permute-done.17.r2), channel_id=1, source_target_pairs={{0,1},{1,0},{2,3},{3,2},{4,5},{5,4},{6,7},{7,6},{8,9},{9,8},{10,11... | collective-permute-start | bytes 405512 | tf_op jit(solution)/shard_map/ppermute | solution.py:552
  160.8 1.4 collective-permute-start.20
  162.2 2.8 %shard_map.118 = f32[12,4,256]{2,1,0:T(4,128)} custom-call(f32[320,128]{1,0:T(8,128)S(1)} %bitcast.17, s32[1,4,32]{2,1,0:T(4,128)S(1)} %get-tuple-element.58.sent, f32[512,128]{1,0:T(8,128)S(1)} %get-tuple-element.83.per_block, s32[1,256]{1,0:T(1,128)S(1)} %get-tuple-element.54.lengths, f32[2,512,128]{2,1,0:T(8,128)S(1)} %get-tuple-element.68.own, ...), custom_call_target="tpu_custom_call" | custom-call | bytes 8000000 | tf_op jit(solution)/shard_map/pallas_call | solution.py:523
  165.0 1.3 shard_map.117
  (32 shorter events, 3.7 us)
Async XLA Ops:
  3.4 23.4 %all-to-all-start = ((f32[32,5,2,128]{3,2,1,0:T(2,128)}), f32[32,5,2,128]{3,2,1,0:T(2,128)S(1)}, u32[]{:S(2)}, u32[]{:S(2)}) async-start(f32[32,5,2,128]{3,2,1,0:T(2,128)} %bitcast.31), calls=%async_computation | async-start | bytes 327680 | tf_op jit(solution)/shard_map/all_to_all | solution.py:559
  15.4 0.8 copy-start
  16.2 0.7 copy-start.1
  16.9 0.7 copy-start.2
  17.6 0.7 copy-start.3
  18.3 0.7 copy-start.4
  26.8 2.1 %collective-permute-start = (f32[320,128]{1,0:T(8,128)S(1)}, f32[320,128]{1,0:T(8,128)S(1)}, u32[]{:S(2)}, u32[]{:S(2)}) collective-permute-start(f32[320,128]{1,0:T(8,128)S(1)} %bitcast.20), channel_id=1, source_target_pairs={{0,1},{1,0},{2,3},{3,2},{4,5},{5,4},{6,7},{7,6},{8,9},{9,8},{10,11... | collective-permute-start | bytes 491528 | tf_op jit(solution)/shard_map/ppermute | solution.py:552
  35.0 1.5 collective-permute-start.1
  46.8 19.0 %collective-permute-start.2 = (f32[4,264,128]{2,1,0:T(8,128)}, f32[4,264,128]{2,1,0:T(8,128)S(1)}, u32[]{:S(2)}, u32[]{:S(2)}) collective-permute-start(f32[4,264,128]{2,1,0:T(8,128)} %get-tuple-element.57), channel_id=1, source_target_pairs={{0,1},{1,0},{2,3},{3,2},{4,5},{5,4},{6,7},{7,6},{8,9},{9,8},{10,11... | collective-permute-start | bytes 1622024 | tf_op jit(solution)/shard_map/ppermute | solution.py:552
  66.3 5.2 %collective-permute-start.3 = (f32[264,128]{1,0:T(8,128)S(1)}, f32[264,128]{1,0:T(8,128)S(1)}, u32[]{:S(2)}, u32[]{:S(2)}) collective-permute-start(f32[264,128]{1,0:T(8,128)S(1)} %get-tuple-element.60), channel_id=1, source_target_pairs={{0,2},{1,3},{2,4},{3,5},{4,6},{5,7},{6,0},{7,1},{8,10},{9,11},{10,... | collective-permute-start | bytes 405512 | tf_op jit(solution)/shard_map/ppermute | solution.py:555
  67.6 6.4 %collective-permute-start.4 = (f32[264,128]{1,0:T(8,128)S(1)}, f32[264,128]{1,0:T(8,128)S(1)}, u32[]{:S(2)}, u32[]{:S(2)}) collective-permute-start(f32[264,128]{1,0:T(8,128)S(1)} %get-tuple-element.61), channel_id=1, source_target_pairs={{0,4},{1,5},{2,6},{3,7},{4,0},{5,1},{6,2},{7,3},{8,12},{9,13},{10,... | collective-permute-start | bytes 405512 | tf_op jit(solution)/shard_map/ppermute | solution.py:555
  70.1 4.2 %collective-permute-start.5 = (f32[264,128]{1,0:T(8,128)S(1)}, f32[264,128]{1,0:T(8,128)S(1)}, u32[]{:S(2)}, u32[]{:S(2)}) collective-permute-start(f32[264,128]{1,0:T(8,128)S(1)} %get-tuple-element.62), channel_id=1, source_target_pairs={{0,6},{1,7},{2,0},{3,1},{4,2},{5,3},{6,4},{7,5},{8,14},{9,15},{10,... | collective-permute-start | bytes 405512 | tf_op jit(solution)/shard_map/ppermute | solution.py:555
  74.4 5.7 %collective-permute-start.8 = (f32[264,128]{1,0:T(8,128)S(1)}, f32[264,128]{1,0:T(8,128)S(1)}, u32[]{:S(2)}, u32[]{:S(2)}) collective-permute-start(f32[264,128]{1,0:T(8,128)S(1)} %shard_map.109.n0), channel_id=1, source_target_pairs={{0,6},{1,7},{2,0},{3,1},{4,2},{5,3},{6,4},{7,5},{8,14},{9,15},{10,... | collective-permute-start | bytes 405512 | tf_op jit(solution)/shard_map/ppermute | solution.py:555
  76.6 5.5 %collective-permute-start.7 = (f32[264,128]{1,0:T(8,128)S(1)}, f32[264,128]{1,0:T(8,128)S(1)}, u32[]{:S(2)}, u32[]{:S(2)}) collective-permute-start(f32[264,128]{1,0:T(8,128)S(1)} %shard_map.109.n0), channel_id=1, source_target_pairs={{0,4},{1,5},{2,6},{3,7},{4,0},{5,1},{6,2},{7,3},{8,12},{9,13},{10,... | collective-permute-start | bytes 405512 | tf_op jit(solution)/shard_map/ppermute | solution.py:555
  77.3 6.1 %collective-permute-start.6 = (f32[264,128]{1,0:T(8,128)S(1)}, f32[264,128]{1,0:T(8,128)S(1)}, u32[]{:S(2)}, u32[]{:S(2)}) collective-permute-start(f32[264,128]{1,0:T(8,128)S(1)} %shard_map.109.n0), channel_id=1, source_target_pairs={{0,2},{1,3},{2,4},{3,5},{4,6},{5,7},{6,0},{7,1},{8,10},{9,11},{10,... | collective-permute-start | bytes 405512 | tf_op jit(solution)/shard_map/ppermute | solution.py:555
  84.5 10.8 %collective-permute-start.9 = (f32[2,512,128]{2,1,0:T(8,128)S(1)}, f32[2,512,128]{2,1,0:T(8,128)S(1)}, u32[]{:S(2)}, u32[]{:S(2)}) collective-permute-start(f32[2,512,128]{2,1,0:T(8,128)S(1)} %get-tuple-element.68.own), channel_id=1, source_target_pairs={{0,1},{1,0},{2,3},{3,2},{4,5},{5,4},{6,7},{7,6},{8,9},{9,8},{10,11... | collective-permute-start | bytes 1572872 | tf_op jit(solution)/shard_map/ppermute | solution.py:552
  90.3 14.3 %all-to-all-start.2 = ((f32[32,5,2,128]{3,2,1,0:T(2,128)}), f32[32,5,2,128]{3,2,1,0:T(2,128)S(1)}, u32[]{:S(2)}, u32[]{:S(2)}) async-start(f32[32,5,2,128]{3,2,1,0:T(2,128)} %bitcast.8), calls=%async_computation.2 | async-start | bytes 327680 | tf_op jit(solution)/shard_map/all_to_all | solution.py:559
  104.5 3.6 %collective-permute-start.10 = (f32[320,128]{1,0:T(8,128)S(1)}, f32[320,128]{1,0:T(8,128)S(1)}, u32[]{:S(2)}, u32[]{:S(2)}) collective-permute-start(f32[320,128]{1,0:T(8,128)S(1)} %bitcast.22), channel_id=1, source_target_pairs={{0,1},{1,0},{2,3},{3,2},{4,5},{5,4},{6,7},{7,6},{8,9},{9,8},{10,11... | collective-permute-start | bytes 491528 | tf_op jit(solution)/shard_map/ppermute | solution.py:552
  114.3 1.5 collective-permute-start.11
  126.2 13.5 %collective-permute-start.12 = (f32[4,264,128]{2,1,0:T(8,128)}, f32[4,264,128]{2,1,0:T(8,128)S(1)}, u32[]{:S(2)}, u32[]{:S(2)}) collective-permute-start(f32[4,264,128]{2,1,0:T(8,128)} %get-tuple-element.77), channel_id=1, source_target_pairs={{0,1},{1,0},{2,3},{3,2},{4,5},{5,4},{6,7},{7,6},{8,9},{9,8},{10,11... | collective-permute-start | bytes 1622024 | tf_op jit(solution)/shard_map/ppermute | solution.py:552
  140.1 6.6 %collective-permute-start.13 = (f32[264,128]{1,0:T(8,128)S(1)}, f32[264,128]{1,0:T(8,128)S(1)}, u32[]{:S(2)}, u32[]{:S(2)}) collective-permute-start(f32[264,128]{1,0:T(8,128)S(1)} %get-tuple-element.79), channel_id=1, source_target_pairs={{0,2},{1,3},{2,4},{3,5},{4,6},{5,7},{6,0},{7,1},{8,10},{9,11},{10,... | collective-permute-start | bytes 405512 | tf_op jit(solution)/shard_map/ppermute | solution.py:555
  140.2 6.5 %collective-permute-start.14 = (f32[264,128]{1,0:T(8,128)S(1)}, f32[264,128]{1,0:T(8,128)S(1)}, u32[]{:S(2)}, u32[]{:S(2)}) collective-permute-start(f32[264,128]{1,0:T(8,128)S(1)} %get-tuple-element.80), channel_id=1, source_target_pairs={{0,4},{1,5},{2,6},{3,7},{4,0},{5,1},{6,2},{7,3},{8,12},{9,13},{10,... | collective-permute-start | bytes 405512 | tf_op jit(solution)/shard_map/ppermute | solution.py:555
  141.6 6.0 %collective-permute-start.15 = (f32[264,128]{1,0:T(8,128)S(1)}, f32[264,128]{1,0:T(8,128)S(1)}, u32[]{:S(2)}, u32[]{:S(2)}) collective-permute-start(f32[264,128]{1,0:T(8,128)S(1)} %get-tuple-element.81), channel_id=1, source_target_pairs={{0,6},{1,7},{2,0},{3,1},{4,2},{5,3},{6,4},{7,5},{8,14},{9,15},{10,... | collective-permute-start | bytes 405512 | tf_op jit(solution)/shard_map/ppermute | solution.py:555
  147.8 7.4 %collective-permute-start.18 = (f32[264,128]{1,0:T(8,128)S(1)}, f32[264,128]{1,0:T(8,128)S(1)}, u32[]{:S(2)}, u32[]{:S(2)}) collective-permute-start(f32[264,128]{1,0:T(8,128)S(1)} %shard_map.116.n0), channel_id=1, source_target_pairs={{0,6},{1,7},{2,0},{3,1},{4,2},{5,3},{6,4},{7,5},{8,14},{9,15},{10,... | collective-permute-start | bytes 405512 | tf_op jit(solution)/shard_map/ppermute | solution.py:555
  149.9 8.4 %collective-permute-start.17 = (f32[264,128]{1,0:T(8,128)S(1)}, f32[264,128]{1,0:T(8,128)S(1)}, u32[]{:S(2)}, u32[]{:S(2)}) collective-permute-start(f32[264,128]{1,0:T(8,128)S(1)} %shard_map.116.n0), channel_id=1, source_target_pairs={{0,4},{1,5},{2,6},{3,7},{4,0},{5,1},{6,2},{7,3},{8,12},{9,13},{10,... | collective-permute-start | bytes 405512 | tf_op jit(solution)/shard_map/ppermute | solution.py:555
  149.9 11.0 %collective-permute-start.16 = (f32[264,128]{1,0:T(8,128)S(1)}, f32[264,128]{1,0:T(8,128)S(1)}, u32[]{:S(2)}, u32[]{:S(2)}) collective-permute-start(f32[264,128]{1,0:T(8,128)S(1)} %shard_map.116.n0), channel_id=1, source_target_pairs={{0,2},{1,3},{2,4},{3,5},{4,6},{5,7},{6,0},{7,1},{8,10},{9,11},{10,... | collective-permute-start | bytes 405512 | tf_op jit(solution)/shard_map/ppermute | solution.py:555
  150.6 14.4 %collective-permute-start.19 = (f32[264,128]{1,0:T(8,128)S(1)}, f32[264,128]{1,0:T(8,128)S(1)}, u32[]{:S(2)}, u32[]{:S(2)}) collective-permute-start(f32[264,128]{1,0:T(8,128)S(1)} %shard_map.116.n0), channel_id=1, source_target_pairs={{0,1},{1,0},{2,3},{3,2},{4,5},{5,4},{6,7},{7,6},{8,9},{9,8},{10,11... | collective-permute-start | bytes 405512 | tf_op jit(solution)/shard_map/ppermute | solution.py:552
  155.2 9.8 %collective-permute-start.22 = (f32[264,128]{1,0:T(8,128)S(1)}, f32[264,128]{1,0:T(8,128)S(1)}, u32[]{:S(2)}, u32[]{:S(2)}) collective-permute-start(f32[264,128]{1,0:T(8,128)S(1)} %collective-permute-done.18.r3), channel_id=1, source_target_pairs={{0,1},{1,0},{2,3},{3,2},{4,5},{5,4},{6,7},{7,6},{8,9},{9,8},{10,11... | collective-permute-start | bytes 405512 | tf_op jit(solution)/shard_map/ppermute | solution.py:552
  158.3 6.7 %collective-permute-start.21 = (f32[264,128]{1,0:T(8,128)S(1)}, f32[264,128]{1,0:T(8,128)S(1)}, u32[]{:S(2)}, u32[]{:S(2)}) collective-permute-start(f32[264,128]{1,0:T(8,128)S(1)} %collective-permute-done.17.r2), channel_id=1, source_target_pairs={{0,1},{1,0},{2,3},{3,2},{4,5},{5,4},{6,7},{7,6},{8,9},{9,8},{10,11... | collective-permute-start | bytes 405512 | tf_op jit(solution)/shard_map/ppermute | solution.py:552
  160.8 4.2 %collective-permute-start.20 = (f32[264,128]{1,0:T(8,128)S(1)}, f32[264,128]{1,0:T(8,128)S(1)}, u32[]{:S(2)}, u32[]{:S(2)}) collective-permute-start(f32[264,128]{1,0:T(8,128)S(1)} %collective-permute-done.16.r1), channel_id=1, source_target_pairs={{0,1},{1,0},{2,3},{3,2},{4,5},{5,4},{6,7},{7,6},{8,9},{9,8},{10,11... | collective-permute-start | bytes 405512 | tf_op jit(solution)/shard_map/ppermute | solution.py:552
where the time goes:
time: 167 us; the launch traced here: 166 us
  Pallas kernels  58.3 us (35%)
  starting transfers between devices  53.6 us (32%)
  blocking collectives  31.6 us (19%)
  waiting for transfers between devices  18.5 us (11%)
  local copies, waits for them, and re-layouts  3.51 us (2%)
    pallas_call x16, Pallas kernels, call(): pl.pallas_call(kernel, out_shape=shapes, in_specs=[far if i in far_in els...  58.3 us
    all_to_all x2, blocking collectives, over_tile(): return lax.all_to_all(v, 'tile', 0, 0, tiled=True).reshape(message)  31.6 us
    ppermute x11, starting transfers between devices, over_core(): return lax.ppermute(v, 'band', [(i, i ^ 1) for i in range(band)])  22.8 us
    all_to_all x2, starting transfers between devices, over_tile(): return lax.all_to_all(v, 'tile', 0, 0, tiled=True).reshape(message)  17.1 us
    ppermute x12, starting transfers between devices, over_x(): lax.ppermute(v, 'band', [(i, (i + 2 * step) % band) for i in range(band)])  13.7 us
    ppermute x12, waiting for transfers between devices, over_x(): lax.ppermute(v, 'band', [(i, (i + 2 * step) % band) for i in range(band)])  11 us
    ppermute x11, waiting for transfers between devices, over_core(): return lax.ppermute(v, 'band', [(i, i ^ 1) for i in range(band)])  4.13 us
    unnamed x10, local copies, waits for them, and re-layouts  3.51 us
  transfers between devices with their start and end apart: 25, of which 12 were waited for; matrix products, arithmetic and copies ran while one was open for 0% of the time, Pallas kernels for 11%

commit v1 on v0

--- a/solution.py
+++ b/solution.py
@@ -167,35 +167,30 @@
     pltpu.sync_copy(message, message_far)
 
 
-def start_kernel(
-    morph, spectra, lengths, counts, sent, land, own, other, colour, alive, table, ablk, *kept
-):
-    _, h = band_place()
-    live, ab, rows = begin(spectra, lengths, counts, colour, own.shape[1])
-    alive[...] = live
-    ablk[...] = ab
-    table[...] = rows
-    for k2 in range(2):
-        own[k2] = morph[k2 ^ (2 * h)] * ab[:, k2 : k2 + 1]
-        other[k2] = morph[(k2 + 2) ^ (2 * h)] * ab[:, k2 + 2 : k2 + 3]
-    for copy, value in zip(kept, (lengths, sent, land)):
-        copy[...] = value[...]
-
-
-def model_kernel(table, own, other, observed_far, out_far, observed, out, sem_in, sem_out):
+def powers(colour, member):
+    sq = colour * colour
+    rows8 = iota((8, sq.shape[1]), 0)
+    power = jnp.zeros((8, sq.shape[1]), F32)
+    for k in range(4):
+        total = jnp.sum(sq[k * KPAD : (k + 1) * KPAD], axis=0, keepdims=True)
+        power = jnp.where(rows8 == k, total, power)
+    hi, lo = halves(power)
+    return lax.dot_general(hi, member, NT, preferred_element_type=F32) + lax.dot_general(
+        lo, member, NT, preferred_element_type=F32
+    )
+
+
+def tile_copies(far, near, sems, out=False):
+    def copy(t):
+        there = slice(None), pl.ds(pl.multiple_of(t * 128, 128), 128)
+        ends = (near.at[there], far.at[there]) if out else (far.at[there], near.at[there])
+        return pltpu.make_async_copy(*ends, sems.at[t])
+
+    return copy
+
+
+def model_loop(table, own, other, observed, out, arrival, leaving):
     channels, blocks, _ = observed.shape
-
-    def there(t):
-        return slice(None), pl.ds(pl.multiple_of(t * 128, 128), 128)
-
-    def arrival(t):
-        return pltpu.make_async_copy(observed_far.at[there(t)], observed.at[there(t)], sem_in.at[t])
-
-    def leaving(t):
-        return pltpu.make_async_copy(out.at[there(t)], out_far.at[there(t)], sem_out.at[t])
-
-    for t in range(blocks // 128):
-        arrival(t).start()
 
     def tile(t, carry):
         arrival(t).wait()
@@ -211,7 +206,86 @@
         return carry
 
     lax.fori_loop(0, blocks // 128, tile, 0)
-    for t in range(blocks // 128):
+
+
+def start_kernel(
+    morph_far,
+    spectra_far,
+    lengths_far,
+    counts_far,
+    sent_far,
+    land_far,
+    observed_far,
+    own,
+    other,
+    colour,
+    alive,
+    table,
+    ablk,
+    lengths,
+    sent,
+    land,
+    wide,
+    resid_far,
+    morph,
+    spectra,
+    counts,
+    observed,
+    resid,
+    sems,
+    sem_in,
+    sem_out,
+):
+    _, h = band_place()
+    near = (lengths, counts, spectra, sent, land, morph)
+    far = (lengths_far, counts_far, spectra_far, sent_far, land_far, morph_far)
+    arrivals = started(
+        [pltpu.make_async_copy(f, n, sems.at[i]) for i, (f, n) in enumerate(zip(far, near))]
+    )
+    arrival = tile_copies(observed_far, observed, sem_in)
+    leaving = tile_copies(resid_far, resid, sem_out, out=True)
+    blocks = own.shape[1]
+    tiles = range(blocks // 128)
+    started([arrival(t) for t in tiles])
+    for c in arrivals[:3]:
+        c.wait()
+    live, ab, rows = begin(spectra, lengths, counts, colour, blocks)
+    alive[...] = live
+    ablk[...] = ab
+    table[...] = rows
+    for c in arrivals[3:]:
+        c.wait()
+    for k2 in range(2):
+        own[k2] = morph[k2 ^ (2 * h)] * ab[:, k2 : k2 + 1]
+        other[k2] = morph[(k2 + 2) ^ (2 * h)] * ab[:, k2 + 2 : k2 + 3]
+    model_loop(table, own, other, observed, resid, arrival, leaving)
+    wide[...] = powers(colour[...], membership_of(lengths[...], blocks))
+    for t in tiles:
+        leaving(t).wait()
+
+
+def model_kernel(
+    table,
+    own,
+    other,
+    colour,
+    lengths,
+    observed_far,
+    wide,
+    resid_far,
+    observed,
+    resid,
+    sem_in,
+    sem_out,
+):
+    arrival = tile_copies(observed_far, observed, sem_in)
+    leaving = tile_copies(resid_far, resid, sem_out, out=True)
+    blocks = own.shape[1]
+    tiles = range(blocks // 128)
+    started([arrival(t) for t in tiles])
+    wide[...] = powers(colour[...], membership_of(lengths[...], blocks))
+    model_loop(table, own, other, observed, resid, arrival, leaving)
+    for t in tiles:
         leaving(t).wait()
 
 
@@ -334,21 +408,46 @@
         gone(c).wait()
 
 
-def grad_kernel(
-    table, own, other, wgt_far, colour, lengths, miss, after, keep, send, per_block, wgt, sems
-):
+def grad_kernel(table, wgt_far, wide, miss, after, keep, send, wgt, sems):
     channels, blocks, _ = wgt.shape
-
-    def arrival(t):
-        there = slice(None), pl.ds(pl.multiple_of(t * 128, 128), 128)
-        return pltpu.make_async_copy(wgt_far.at[there], wgt.at[there], sems.at[t])
-
-    for t in range(blocks // 128):
-        arrival(t).start()
+    quarter = blocks // 4
+    arrival = tile_copies(wgt_far, wgt, sems)
+    started([arrival(t) for t in range(4)])
+    for q in range(4):
+        w = wide[:, q * quarter : (q + 1) * quarter]
+        m = miss[0:1, q * quarter : (q + 1) * quarter]
+        r = iota((8, quarter), 0)
+        first = jnp.where(r == 0, m, jnp.where(r == 1, w[0:1], jnp.where(r == 2, w[1:2], 0.0)))
+        second = jnp.where(r == 0, m, jnp.where(r == 1, w[2:3], jnp.where(r == 2, w[3:4], 0.0)))
+        keep[q, pl.ds(2 * quarter, EXTRA), :] = first
+        send[q, pl.ds(2 * quarter, EXTRA), :] = second
+
+    def shapes(q, carry):
+        arrival(q).wait()
+        for half in range(2):
+            rows = pl.ds(pl.multiple_of(q * quarter + half * 64, 64), 64)
+            cb = table[rows, :]
+            gs = [None] * 4
+            for c in range(channels):
+                wt = wgt[c, rows, :]
+                for k in range(4):
+                    term = cb[:, k * KPAD + c : k * KPAD + c + 1] * wt
+                    gs[k] = term if c == 0 else gs[k] + term
+            for k2 in range(2):
+                keep[q, pl.ds(k2 * quarter + half * 64, 64), :] = gs[k2]
+                send[q, pl.ds(k2 * quarter + half * 64, 64), :] = gs[k2 + 2]
+        return carry
+
+    lax.fori_loop(0, 4, shapes, 0)
+
+
+def product_kernel(own, other, wgt_far, per_block, wgt, sems):
+    channels, blocks, _ = wgt.shape
     lane = iota((128, 128), 1)
-    quarter = blocks // 4
-
-    def colours(t, carry):
+    arrival = tile_copies(wgt_far, wgt, sems)
+    started([arrival(t) for t in range(blocks // 128)])
+
+    def tile(t, carry):
         arrival(t).wait()
         rows = pl.ds(pl.multiple_of(t * 128, 128), 128)
         sh = [own[0, rows, :], own[1, rows, :], other[0, rows, :], other[1, rows, :]]
@@ -361,43 +460,7 @@
         per_block[rows, :] = pb
         return carry
 
-    lax.fori_loop(0, blocks // 128, colours, 0)
-
-    def shapes(t, carry):
-        q, inside = t // 2, pl.multiple_of((t % 2) * 64, 64)
-        rows = pl.ds(pl.multiple_of(t * 64, 64), 64)
-        cb = table[rows, :]
-        gs = [None] * 4
-        for c in range(channels):
-            wt = wgt[c, rows, :]
-            for k in range(4):
-                term = cb[:, k * KPAD + c : k * KPAD + c + 1] * wt
-                gs[k] = term if c == 0 else gs[k] + term
-        for k2 in range(2):
-            keep[q, pl.ds(k2 * quarter + inside, 64), :] = gs[k2]
-            send[q, pl.ds(k2 * quarter + inside, 64), :] = gs[k2 + 2]
-        return carry
-
-    lax.fori_loop(0, blocks // 64, shapes, 0)
-    member = membership_of(lengths[...], blocks)
-    sq = colour[...] * colour[...]
-    rows8 = iota((8, sq.shape[1]), 0)
-    power = jnp.zeros((8, sq.shape[1]), F32)
-    for k in range(4):
-        total = jnp.sum(sq[k * KPAD : (k + 1) * KPAD], axis=0, keepdims=True)
-        power = jnp.where(rows8 == k, total, power)
-    hi, lo = halves(power)
-    wide = lax.dot_general(hi, member, NT, preferred_element_type=F32) + lax.dot_general(
-        lo, member, NT, preferred_element_type=F32
-    )
-    for q in range(4):
-        w = wide[:, q * quarter : (q + 1) * quarter]
-        m = miss[0:1, q * quarter : (q + 1) * quarter]
-        r = iota((8, quarter), 0)
-        first = jnp.where(r == 0, m, jnp.where(r == 1, w[0:1], jnp.where(r == 2, w[1:2], 0.0)))
-        second = jnp.where(r == 0, m, jnp.where(r == 1, w[2:3], jnp.where(r == 2, w[3:4], 0.0)))
-        keep[q, pl.ds(2 * quarter, EXTRA), :] = first
-        send[q, pl.ds(2 * quarter, EXTRA), :] = second
+    lax.fori_loop(0, blocks // 128, tile, 0)
 
 
 def merge_kernel(arrived, keep, came, sent, p0, p1, p2, p3, scat):
@@ -587,7 +650,8 @@
         far_in=range(5),
         far_out=(0,),
     )
-    own, other, colour, alive, table, ablk, lengths, sent, land = call(
+    tiles = blocks // 128
+    own, other, colour, alive, table, ablk, lengths, sent, land, wide, resid = call(
         start_kernel,
         [
             pair,
@@ -599,21 +663,46 @@
             kept(blend_blocks),
             kept(sent_blocks),
             kept(landing_blocks),
+            (8, blocks),
+            observed.shape,
         ],
-        (morphology, spectra, blend_blocks, counts, sent_blocks, landing_blocks),
+        (
+            morphology,
+            spectra,
+            blend_blocks,
+            counts,
+            sent_blocks,
+            landing_blocks,
+            observed,
+        ),
+        scratch=(
+            pltpu.VMEM(morphology.shape, F32),
+            pltpu.VMEM(spectra.shape, F32),
+            pltpu.VMEM(counts.shape, jnp.int32),
+            cube,
+            cube,
+            dma(6),
+            dma(tiles),
+            dma(tiles),
+        ),
+        cost=20e6,
+        limit=67_043_328,
+        far_in=range(7),
+        far_out=(10,),
     )
     for iteration in range(ITERS):
         last = iteration == ITERS - 1
         mine = over_tile(leaving)
-        resid = call(
-            model_kernel,
-            observed.shape,
-            (table, own, other, observed),
-            scratch=(cube, cube, dma(blocks // 128), dma(blocks // 128)),
-            cost=16e6,
-            far_in=(3,),
-            far_out=(0,),
-        )
+        if iteration:
+            wide, resid = call(
+                model_kernel,
+                [(8, blocks), observed.shape],
+                (table, own, other, colour, lengths, observed),
+                scratch=(cube, cube, dma(tiles), dma(tiles)),
+                cost=16e6,
+                far_in=(5,),
+                far_out=(1,),
+            )
         mine, resid = lax.optimization_barrier((mine, resid))
         partner = over_core(mine)
         wgt, bkeep, bsend, miss = call(
@@ -639,13 +728,13 @@
         )
         returning = bkeep + over_core(bsend)
         back = over_tile(returning)
-        gkeep, gsend, per_block = call(
+        gkeep, gsend = call(
             grad_kernel,
-            [(4,) + piece, (4,) + piece, table_rows],
-            (table, own, other, wgt, colour, lengths, miss, returning),
-            scratch=(cube, dma(blocks // 128)),
-            cost=30e6,
-            far_in=(3, 7),
+            [(4,) + piece, (4,) + piece],
+            (table, wgt, wide, miss, returning),
+            scratch=(cube, dma(tiles)),
+            cost=16e6,
+            far_in=(1, 4),
         )
         gcame = over_core(gsend)
         p0, p1, p2, p3 = call(
@@ -656,6 +745,14 @@
             limit=SMALL,
         )
         r1, r2, r3 = (over_x(v, s) for s, v in ((1, p1), (2, p2), (3, p3)))
+        per_block = call(
+            product_kernel,
+            table_rows,
+            (own, other, wgt),
+            scratch=(cube, dma(tiles)),
+            cost=16e6,
+            far_in=(2,),
+        )
         colour_args = (back, sent, per_block, lengths, own, other, colour, alive)
         if last:
             new_colour = call(

time: 167 us -> 161 us (0.964)
  waiting for transfers between devices: 18.5 us -> 14.6 us
  local copies, waits for them, and re-layouts: 3.51 us -> 0.71 us
  blocking collectives: 31.6 us -> 29.7 us
  Pallas kernels: 58.3 us -> 60 us
    ppermute x12, waiting for transfers between devices: 11 us -> 6.41 us  [over_x(): lax.ppermute(v, 'band', [(i, (i + 2 * step) % band) for i in range(band)])]
    unnamed x10 -> x22, local copies, waits for them, and re-layouts: 3.51 us -> 0.71 us
    ppermute x12, starting transfers between devices: 13.7 us -> 15.6 us  [over_x(): lax.ppermute(v, 'band', [(i, (i + 2 * step) % band) for i in range(band)])]
    all_to_all x2, blocking collectives: 31.6 us -> 29.7 us  [over_tile(): return lax.all_to_all(v, 'tile', 0, 0, tiled=True).reshape(message)]
    pallas_call x16 -> x17, Pallas kernels: 58.3 us -> 60 us  [call(): pl.pallas_call(kernel, out_shape=shapes, in_specs=[far if i in far_in els...]
  transfers between devices with their start and end apart: 25 -> 25, of which waited for: 12 -> 12; matrix products, arithmetic and copies ran while one was open for 0% -> 0% of each run, Pallas kernels for 11% -> 18%
where the time goes in v1:
time: 161 us
  Pallas kernels  60 us (37%)
  starting transfers between devices  54.9 us (34%)
  blocking collectives  29.7 us (18%)
  waiting for transfers between devices  14.6 us (9%)
    pallas_call x17, Pallas kernels, call(): pl.pallas_call(kernel, out_shape=shapes, in_specs=[far if i in far_in els...  60 us
    all_to_all x2, blocking collectives, over_tile(): return lax.all_to_all(v, 'tile', 0, 0, tiled=True).reshape(message)  29.7 us
    ppermute x11, starting transfers between devices, over_core(): return lax.ppermute(v, 'band', [(i, i ^ 1) for i in range(band)])  22.8 us
    all_to_all x2, starting transfers between devices, over_tile(): return lax.all_to_all(v, 'tile', 0, 0, tiled=True).reshape(message)  16.5 us
    ppermute x12, starting transfers between devices, over_x(): lax.ppermute(v, 'band', [(i, (i + 2 * step) % band) for i in range(band)])  15.6 us
    ppermute x12, waiting for transfers between devices, over_x(): lax.ppermute(v, 'band', [(i, (i + 2 * step) % band) for i in range(band)])  6.41 us
    ppermute x11, waiting for transfers between devices, over_core(): return lax.ppermute(v, 'band', [(i, i ^ 1) for i in range(band)])  4.34 us
    all_to_all x2, waiting for transfers between devices, over_tile(): return lax.all_to_all(v, 'tile', 0, 0, tiled=True).reshape(message)  3.8 us
  transfers between devices with their start and end apart: 25, of which 12 were waited for; matrix products, arithmetic and copies ran while one was open for 0% of the time, Pallas kernels for 18%

profile of v1, /device:TPU:1, one launch (start us, length us, event | category | flops | bytes accessed | tf_op | source)
XLA Modules:
  0.0 160.8 jit_solution(6575412290650279350)
XLA Ops:
  0.6 2.7 %shard_map.103 = f32[320,128]{1,0:T(8,128)} custom-call(f32[4,512,128]{2,1,0:T(8,128)} %morph_far.3, f32[12,4,256]{2,1,0:T(4,128)} %bitcast.23, s32[1,256]{1,0:T(1,128)} %lengths_far.3, s32[1,256]{1,0:T(1,128)} %bitcast.28, s32[1,4,32]{2,1,0:T(4,128)} %bitcast.26), custom_call_target="tpu_custom_call" | custom-call | bytes 3000000 | tf_op jit(solution)/shard_map/pallas_call | solution.py:586
  3.4 12.2 %all-to-all-start = ((f32[32,5,2,128]{3,2,1,0:T(2,128)}), f32[32,5,2,128]{3,2,1,0:T(2,128)}, u32[]{:S(2)}, u32[]{:S(2)}) async-start(f32[32,5,2,128]{3,2,1,0:T(2,128)} %bitcast.22), calls=%async_computation | async-start | bytes 327680 | tf_op jit(solution)/shard_map/all_to_all | solution.py:622
  15.5 8.6 %shard_map.104 = (f32[2,512,128]{2,1,0:T(8,128)}, f32[2,512,128]{2,1,0:T(8,128)}, f32[64,256]{1,0:T(8,128)}, f32[8,256]{1,0:T(8,128)}, f32[512,128]{1,0:T(8,128)...) custom-call(f32[4,512,128]{2,1,0:T(8,128)} %morph_far.3, ...), custom_call_target="tpu_custom_call" | custom-call | bytes 20000000 | tf_op jit(solution)/shard_map/pallas_call | solution.py:586
  24.2 0.7 all-to-all-done
  24.9 2.4 %collective-permute-start = (f32[320,128]{1,0:T(8,128)}, f32[320,128]{1,0:T(8,128)S(1)}, u32[]{:S(2)}, u32[]{:S(2)}) collective-permute-start(f32[320,128]{1,0:T(8,128)} %bitcast.4.mine), channel_id=1, source_target_pairs={{0,1},{1,0},{2,3},{3,2},{4,5},{5,4},{6,7},{7,6},{8,9},{9,8},{10,11... | collective-permute-start | bytes 491528 | tf_op jit(solution)/shard_map/ppermute | solution.py:615
  27.3 1.2 collective-permute-done.partner
  28.5 0.7 copy-done.9
  29.2 7.1 %shard_map.105 = (f32[12,512,128]{2,1,0:T(8,128)}, f32[320,128]{1,0:T(8,128)S(1)}, f32[320,128]{1,0:T(8,128)S(1)}, f32[8,512]{1,0:T(8,128)S(1)}) custom-call(f32[320,128]{1,0:T(8,128)} %bitcast.4.mine, f32[320,128]{1,0:T(8,128)S(1)} %collective-permute-done.partner, f32[12,512,128]{2,1,0:T(8,128)} %get-tuple-element.48.resid_far, ...), custom_call_target="tpu_custom_call" | custom-call | bytes 14000000 | tf_op jit(solution)/shard_map/pallas_call | solution.py:586
  36.7 1.0 collective-permute-done.1
  37.8 5.5 %shard_map.106 = (f32[4,264,128]{2,1,0:T(8,128)S(1)}, f32[4,264,128]{2,1,0:T(8,128)S(1)}) custom-call(f32[512,128]{1,0:T(8,128)S(1)} %copy-done.3, f32[12,512,128]{2,1,0:T(8,128)} %get-tuple-element.53.wgt_far, f32[8,512]{1,0:T(8,128)S(1)} %copy-done.7, f32[8,512]{1,0:T(8,128)S(1)} %get-tuple-element.55.miss, f32[320,128]{1,0:T(8,128)S(1)} %add.6.after), custom_call_target="tpu_custom_call" | custom-call | bytes 16000000 | tf_op jit(solution)/shard_map/pallas_call | solution.py:586
  43.7 16.5 %all_to_all.20 = f32[32,5,2,128]{3,2,1,0:T(2,128)S(1)} all-to-all(f32[32,5,2,128]{3,2,1,0:T(2,128)S(1)} %bitcast.15), channel_id=1, replica_groups=mesh['tile'=32,'band'=8] {'tile'}, dimensions={0} | all-to-all | bytes 327680 | tf_op jit(solution)/shard_map/all_to_all | solution.py:622
  60.2 0.5 shard_map.107
  60.7 1.3 collective-permute-start.3
  62.0 2.5 %collective-permute-start.4 = (f32[264,128]{1,0:T(8,128)S(1)}, f32[264,128]{1,0:T(8,128)S(1)}, u32[]{:S(2)}, u32[]{:S(2)}) collective-permute-start(f32[264,128]{1,0:T(8,128)S(1)} %get-tuple-element.61), channel_id=1, source_target_pairs={{0,4},{1,5},{2,6},{3,7},{4,0},{5,1},{6,2},{7,3},{8,12},{9,13},{10,... | collective-permute-start | bytes 405512 | tf_op jit(solution)/shard_map/ppermute | solution.py:618
  64.5 1.2 collective-permute-start.5
  65.9 2.5 %collective-permute-done.4.r2 = f32[264,128]{1,0:T(8,128)S(1)} collective-permute-done((f32[264,128]{1,0:T(8,128)S(1)}, f32[264,128]{1,0:T(8,128)S(1)}, u32[]{:S(2)}, u32[]{:S(2)}) %collective-permute-start.4) | collective-permute-done | bytes 135200 | tf_op jit(solution)/shard_map/ppermute | solution.py:618
  68.8 2.1 %collective-permute-start.8 = (f32[264,128]{1,0:T(8,128)S(1)}, f32[264,128]{1,0:T(8,128)S(1)}, u32[]{:S(2)}, u32[]{:S(2)}) collective-permute-start(f32[264,128]{1,0:T(8,128)S(1)} %shard_map.108.n0), channel_id=1, source_target_pairs={{0,6},{1,7},{2,0},{3,1},{4,2},{5,3},{6,4},{7,5},{8,14},{9,15},{10,... | collective-permute-start | bytes 405512 | tf_op jit(solution)/shard_map/ppermute | solution.py:618
  71.0 0.8 collective-permute-start.7
  72.1 4.7 %shard_map.109.per_block = f32[512,128]{1,0:T(8,128)S(1)} custom-call(f32[2,512,128]{2,1,0:T(8,128)S(1)} %copy-done, f32[2,512,128]{2,1,0:T(8,128)S(1)} %copy-done.1, f32[12,512,128]{2,1,0:T(8,128)} %get-tuple-element.53.wgt_far), custom_call_target="tpu_custom_call" | custom-call | bytes 16000000 | tf_op jit(solution)/shard_map/pallas_call | solution.py:586
  76.9 2.4 %shard_map.110 = (f32[64,256]{1,0:T(8,128)S(1)}, f32[512,128]{1,0:T(8,128)S(1)}) custom-call(f32[320,128]{1,0:T(8,128)S(1)} %bitcast.19, s32[1,4,32]{2,1,0:T(4,128)S(1)} %copy-done.5, f32[512,128]{1,0:T(8,128)S(1)} %shard_map.109.per_block, s32[1,256]{1,0:T(1,128)S(1)} %copy-done.8, f32[2,512,128]{2,1,0:T(8,128)S(1)} %copy-done, ...), custom_call_target="tpu_custom_call" | custom-call | bytes 8000000 | tf_op jit(solution)/shard_map/pallas_call | solution.py:586
  79.3 1.1 shard_map.111
  80.4 4.9 %collective-permute-start.9 = (f32[2,512,128]{2,1,0:T(8,128)S(1)}, f32[2,512,128]{2,1,0:T(8,128)S(1)}, u32[]{:S(2)}, u32[]{:S(2)}) collective-permute-start(f32[2,512,128]{2,1,0:T(8,128)S(1)} %get-tuple-element.71.own), channel_id=1, source_target_pairs={{0,1},{1,0},{2,3},{3,2},{4,5},{5,4},{6,7},{7,6},{8,9},{9,8},{10,11... | collective-permute-start | bytes 1572872 | tf_op jit(solution)/shard_map/ppermute | solution.py:615
  85.4 4.3 %all-to-all-start.2 = ((f32[32,5,2,128]{3,2,1,0:T(2,128)}), f32[32,5,2,128]{3,2,1,0:T(2,128)S(1)}, u32[]{:S(2)}, u32[]{:S(2)}) async-start(f32[32,5,2,128]{3,2,1,0:T(2,128)} %bitcast.8), calls=%async_computation.2 | async-start | bytes 327680 | tf_op jit(solution)/shard_map/all_to_all | solution.py:622
  89.7 6.1 %shard_map.112 = (f32[8,512]{1,0:T(8,128)S(1)}, f32[12,512,128]{2,1,0:T(8,128)}) custom-call(f32[512,128]{1,0:T(8,128)S(1)} %get-tuple-element.69.table, f32[2,512,128]{2,1,0:T(8,128)S(1)} %get-tuple-element.71.own, f32[2,512,128]{2,1,0:T(8,128)S(1)} %collective-permute-done.9.other, f32[64,256]{1,0:T(8,128)S(1)} %get-tuple-element.72.colour, ...), custom_call_target="tpu_custom_call" | custom-call | bytes 16000000 | tf_op jit(solution)/shard_map/pallas_call | solution.py:586
  95.9 3.1 %all-to-all-done.2 = f32[32,5,2,128]{3,2,1,0:T(2,128)S(1)} async-done(((f32[32,5,2,128]{3,2,1,0:T(2,128)}), f32[32,5,2,128]{3,2,1,0:T(2,128)S(1)}, u32[]{:S(2)}, u32[]{:S(2)}) %all-to-all-start.2) | async-done | bytes 163872 | tf_op jit(solution)/shard_map/all_to_all | solution.py:622
  99.0 2.6 %collective-permute-start.10 = (f32[320,128]{1,0:T(8,128)S(1)}, f32[320,128]{1,0:T(8,128)S(1)}, u32[]{:S(2)}, u32[]{:S(2)}) collective-permute-start(f32[320,128]{1,0:T(8,128)S(1)} %bitcast.20), channel_id=1, source_target_pairs={{0,1},{1,0},{2,3},{3,2},{4,5},{5,4},{6,7},{7,6},{8,9},{9,8},{10,11... | collective-permute-start | bytes 491528 | tf_op jit(solution)/shard_map/ppermute | solution.py:615
  101.6 1.0 collective-permute-done.10.partner
  102.6 6.1 %shard_map.113 = (f32[12,512,128]{2,1,0:T(8,128)}, f32[320,128]{1,0:T(8,128)S(1)}, f32[320,128]{1,0:T(8,128)S(1)}, f32[8,512]{1,0:T(8,128)S(1)}) custom-call(f32[320,128]{1,0:T(8,128)S(1)} %bitcast.21, f32[320,128]{1,0:T(8,128)S(1)} %collective-permute-done.10.partner, f32[12,512,128]{2,1,0:T(8,128)} %get-tuple-element.75.resid_far, ...), custom_call_target="tpu_custom_call" | custom-call | bytes 14000000 | tf_op jit(solution)/shard_map/pallas_call | solution.py:586
  108.7 0.5 collective-permute-start.11
  109.2 1.0 collective-permute-done.11
  110.2 5.4 %shard_map.114 = (f32[4,264,128]{2,1,0:T(8,128)S(1)}, f32[4,264,128]{2,1,0:T(8,128)S(1)}) custom-call(f32[512,128]{1,0:T(8,128)S(1)} %get-tuple-element.69.table, f32[12,512,128]{2,1,0:T(8,128)} %get-tuple-element.78.wgt_far, f32[8,512]{1,0:T(8,128)S(1)} %get-tuple-element.79.wide, f32[8,512]{1,0:T(8,128)S(1)} %get-tuple-element.80.miss, ...), custom_call_target="tpu_custom_call" | custom-call | bytes 16000000 | tf_op jit(solution)/shard_map/pallas_call | solution.py:586
  115.6 0.5 collective-permute-start.12
  116.1 13.2 %all_to_all.21 = f32[32,5,2,128]{3,2,1,0:T(2,128)S(1)} all-to-all(f32[32,5,2,128]{3,2,1,0:T(2,128)S(1)} %bitcast.14), channel_id=1, replica_groups=mesh['tile'=32,'band'=8] {'tile'}, dimensions={0} | all-to-all | bytes 327680 | tf_op jit(solution)/shard_map/all_to_all | solution.py:622
  129.3 0.5 shard_map.115
  129.8 1.8 %collective-permute-start.13 = (f32[264,128]{1,0:T(8,128)S(1)}, f32[264,128]{1,0:T(8,128)S(1)}, u32[]{:S(2)}, u32[]{:S(2)}) collective-permute-start(f32[264,128]{1,0:T(8,128)S(1)} %get-tuple-element.84), channel_id=1, source_target_pairs={{0,2},{1,3},{2,4},{3,5},{4,6},{5,7},{6,0},{7,1},{8,10},{9,11},{10,... | collective-permute-start | bytes 405512 | tf_op jit(solution)/shard_map/ppermute | solution.py:618
  131.6 1.7 %collective-permute-start.14 = (f32[264,128]{1,0:T(8,128)S(1)}, f32[264,128]{1,0:T(8,128)S(1)}, u32[]{:S(2)}, u32[]{:S(2)}) collective-permute-start(f32[264,128]{1,0:T(8,128)S(1)} %get-tuple-element.85), channel_id=1, source_target_pairs={{0,4},{1,5},{2,6},{3,7},{4,0},{5,1},{6,2},{7,3},{8,12},{9,13},{10,... | collective-permute-start | bytes 405512 | tf_op jit(solution)/shard_map/ppermute | solution.py:618
  133.3 0.8 collective-permute-start.15
  134.1 0.9 collective-permute-done.13.r1
  135.0 2.2 %collective-permute-done.14.r2 = f32[264,128]{1,0:T(8,128)S(1)} collective-permute-done((f32[264,128]{1,0:T(8,128)S(1)}, f32[264,128]{1,0:T(8,128)S(1)}, u32[]{:S(2)}, u32[]{:S(2)}) %collective-permute-start.14) | collective-permute-done | bytes 135200 | tf_op jit(solution)/shard_map/ppermute | solution.py:618
  137.7 2.0 %collective-permute-start.18 = (f32[264,128]{1,0:T(8,128)S(1)}, f32[264,128]{1,0:T(8,128)S(1)}, u32[]{:S(2)}, u32[]{:S(2)}) collective-permute-start(f32[264,128]{1,0:T(8,128)S(1)} %shard_map.116.n0), channel_id=1, source_target_pairs={{0,6},{1,7},{2,0},{3,1},{4,2},{5,3},{6,4},{7,5},{8,14},{9,15},{10,... | collective-permute-start | bytes 405512 | tf_op jit(solution)/shard_map/ppermute | solution.py:618
  139.7 1.2 collective-permute-start.17
  140.8 4.1 %collective-permute-start.19 = (f32[264,128]{1,0:T(8,128)S(1)}, f32[264,128]{1,0:T(8,128)S(1)}, u32[]{:S(2)}, u32[]{:S(2)}) collective-permute-start(f32[264,128]{1,0:T(8,128)S(1)} %shard_map.116.n0), channel_id=1, source_target_pairs={{0,1},{1,0},{2,3},{3,2},{4,5},{5,4},{6,7},{7,6},{8,9},{9,8},{10,11... | collective-permute-start | bytes 405512 | tf_op jit(solution)/shard_map/ppermute | solution.py:615
  145.0 2.4 %collective-permute-start.22 = (f32[264,128]{1,0:T(8,128)S(1)}, f32[264,128]{1,0:T(8,128)S(1)}, u32[]{:S(2)}, u32[]{:S(2)}) collective-permute-start(f32[264,128]{1,0:T(8,128)S(1)} %collective-permute-done.18.r3), channel_id=1, source_target_pairs={{0,1},{1,0},{2,3},{3,2},{4,5},{5,4},{6,7},{7,6},{8,9},{9,8},{10,11... | collective-permute-start | bytes 405512 | tf_op jit(solution)/shard_map/ppermute | solution.py:615
  147.4 3.2 %collective-permute-start.21 = (f32[264,128]{1,0:T(8,128)S(1)}, f32[264,128]{1,0:T(8,128)S(1)}, u32[]{:S(2)}, u32[]{:S(2)}) collective-permute-start(f32[264,128]{1,0:T(8,128)S(1)} %collective-permute-done.17.r2), channel_id=1, source_target_pairs={{0,1},{1,0},{2,3},{3,2},{4,5},{5,4},{6,7},{7,6},{8,9},{9,8},{10,11... | collective-permute-start | bytes 405512 | tf_op jit(solution)/shard_map/ppermute | solution.py:615
  150.6 1.4 collective-permute-start.20
  152.0 4.7 %shard_map.118.per_block = f32[512,128]{1,0:T(8,128)S(1)} custom-call(f32[2,512,128]{2,1,0:T(8,128)S(1)} %get-tuple-element.71.own, f32[2,512,128]{2,1,0:T(8,128)S(1)} %collective-permute-done.9.other, f32[12,512,128]{2,1,0:T(8,128)} %get-tuple-element.78.wgt_far), custom_call_target="tpu_custom_call" | custom-call | bytes 16000000 | tf_op jit(solution)/shard_map/pallas_call | solution.py:586
  156.7 2.8 %shard_map.119 = f32[12,4,256]{2,1,0:T(4,128)} custom-call(f32[320,128]{1,0:T(8,128)S(1)} %bitcast.17, s32[1,4,32]{2,1,0:T(4,128)S(1)} %copy-done.5, f32[512,128]{1,0:T(8,128)S(1)} %shard_map.118.per_block, s32[1,256]{1,0:T(1,128)S(1)} %copy-done.8, f32[2,512,128]{2,1,0:T(8,128)S(1)} %get-tuple-element.71.own, ...), custom_call_target="tpu_custom_call" | custom-call | bytes 8000000 | tf_op jit(solution)/shard_map/pallas_call | solution.py:586
  159.5 1.3 shard_map.117
  (45 shorter events, 2.6 us)
Async XLA Ops:
  3.4 21.5 %all-to-all-start = ((f32[32,5,2,128]{3,2,1,0:T(2,128)}), f32[32,5,2,128]{3,2,1,0:T(2,128)}, u32[]{:S(2)}, u32[]{:S(2)}) async-start(f32[32,5,2,128]{3,2,1,0:T(2,128)} %bitcast.22), calls=%async_computation | async-start | bytes 327680 | tf_op jit(solution)/shard_map/all_to_all | solution.py:622
  24.9 3.6 %collective-permute-start = (f32[320,128]{1,0:T(8,128)}, f32[320,128]{1,0:T(8,128)S(1)}, u32[]{:S(2)}, u32[]{:S(2)}) collective-permute-start(f32[320,128]{1,0:T(8,128)} %bitcast.4.mine), channel_id=1, source_target_pairs={{0,1},{1,0},{2,3},{3,2},{4,5},{5,4},{6,7},{7,6},{8,9},{9,8},{10,11... | collective-permute-start | bytes 491528 | tf_op jit(solution)/shard_map/ppermute | solution.py:615
  28.5 0.7 copy-start.9
  29.2 8.6 %copy-start.3 = (f32[512,128]{1,0:T(8,128)S(1)}, f32[512,128]{1,0:T(8,128)}, u32[]{:S(2)}) copy-start(f32[512,128]{1,0:T(8,128)} %get-tuple-element.52.table) | copy-start | bytes 786436
  29.2 8.6 %copy-start.7 = (f32[8,512]{1,0:T(8,128)S(1)}, f32[8,512]{1,0:T(8,128)}, u32[]{:S(2)}) copy-start(f32[8,512]{1,0:T(8,128)} %get-tuple-element.54.wide) | copy-start | bytes 49156
  36.2 24.0 %copy-start.5 = (s32[1,4,32]{2,1,0:T(4,128)S(1)}, s32[1,4,32]{2,1,0:T(4,128)}, u32[]{:S(2)}) copy-start(s32[1,4,32]{2,1,0:T(4,128)} %get-tuple-element.58.sent) | copy-start | bytes 1540
  36.3 32.4 %copy-start = (f32[2,512,128]{2,1,0:T(8,128)S(1)}, f32[2,512,128]{2,1,0:T(8,128)}, u32[]{:S(2)}) copy-start(f32[2,512,128]{2,1,0:T(8,128)} %get-tuple-element.63.own) | copy-start | bytes 1572868
  36.3 32.4 %copy-start.2 = (f32[512,128]{1,0:T(8,128)S(1)}, f32[512,128]{1,0:T(8,128)}, u32[]{:S(2)}) copy-start(f32[512,128]{1,0:T(8,128)} %get-tuple-element.64.ablk) | copy-start | bytes 786436
  36.3 1.5 collective-permute-start.1
  37.8 34.3 %copy-start.1 = (f32[2,512,128]{2,1,0:T(8,128)S(1)}, f32[2,512,128]{2,1,0:T(8,128)}, u32[]{:S(2)}) copy-start(f32[2,512,128]{2,1,0:T(8,128)} %get-tuple-element.65.other) | copy-start | bytes 1572868
  43.3 16.9 %collective-permute-start.2 = (f32[4,264,128]{2,1,0:T(8,128)S(1)}, f32[4,264,128]{2,1,0:T(8,128)S(1)}, u32[]{:S(2)}, u32[]{:S(2)}) collective-permute-start(f32[4,264,128]{2,1,0:T(8,128)S(1)} %get-tuple-element.57), channel_id=1, source_target_pairs={{0,1},{1,0},{2,3},{3,2},{4,5},{5,4},{6,7},{7,6},{8,9},{9,8},{10,11... | collective-permute-start | bytes 1622024 | tf_op jit(solution)/shard_map/ppermute | solution.py:615
  60.7 16.2 %copy-start.4 = (f32[64,256]{1,0:T(8,128)S(1)}, f32[64,256]{1,0:T(8,128)}, u32[]{:S(2)}) copy-start(f32[64,256]{1,0:T(8,128)} %get-tuple-element.67.colour) | copy-start | bytes 196612
  60.7 16.2 %copy-start.6 = (f32[8,256]{1,0:T(8,128)S(1)}, f32[8,256]{1,0:T(8,128)}, u32[]{:S(2)}) copy-start(f32[8,256]{1,0:T(8,128)} %get-tuple-element.68.alive) | copy-start | bytes 24580
  60.7 16.2 %copy-start.8 = (s32[1,256]{1,0:T(1,128)S(1)}, s32[1,256]{1,0:T(1,128)}, u32[]{:S(2)}) copy-start(s32[1,256]{1,0:T(1,128)} %get-tuple-element.66.lengths) | copy-start | bytes 3076
  60.7 5.2 %collective-permute-start.3 = (f32[264,128]{1,0:T(8,128)S(1)}, f32[264,128]{1,0:T(8,128)S(1)}, u32[]{:S(2)}, u32[]{:S(2)}) collective-permute-start(f32[264,128]{1,0:T(8,128)S(1)} %get-tuple-element.60), channel_id=1, source_target_pairs={{0,2},{1,3},{2,4},{3,5},{4,6},{5,7},{6,0},{7,1},{8,10},{9,11},{10,... | collective-permute-start | bytes 405512 | tf_op jit(solution)/shard_map/ppermute | solution.py:618
  62.0 6.4 %collective-permute-start.4 = (f32[264,128]{1,0:T(8,128)S(1)}, f32[264,128]{1,0:T(8,128)S(1)}, u32[]{:S(2)}, u32[]{:S(2)}) collective-permute-start(f32[264,128]{1,0:T(8,128)S(1)} %get-tuple-element.61), channel_id=1, source_target_pairs={{0,4},{1,5},{2,6},{3,7},{4,0},{5,1},{6,2},{7,3},{8,12},{9,13},{10,... | collective-permute-start | bytes 405512 | tf_op jit(solution)/shard_map/ppermute | solution.py:618
  64.5 4.2 %collective-permute-start.5 = (f32[264,128]{1,0:T(8,128)S(1)}, f32[264,128]{1,0:T(8,128)S(1)}, u32[]{:S(2)}, u32[]{:S(2)}) collective-permute-start(f32[264,128]{1,0:T(8,128)S(1)} %get-tuple-element.62), channel_id=1, source_target_pairs={{0,6},{1,7},{2,0},{3,1},{4,2},{5,3},{6,4},{7,5},{8,14},{9,15},{10,... | collective-permute-start | bytes 405512 | tf_op jit(solution)/shard_map/ppermute | solution.py:618
  68.8 10.4 %collective-permute-start.8 = (f32[264,128]{1,0:T(8,128)S(1)}, f32[264,128]{1,0:T(8,128)S(1)}, u32[]{:S(2)}, u32[]{:S(2)}) collective-permute-start(f32[264,128]{1,0:T(8,128)S(1)} %shard_map.108.n0), channel_id=1, source_target_pairs={{0,6},{1,7},{2,0},{3,1},{4,2},{5,3},{6,4},{7,5},{8,14},{9,15},{10,... | collective-permute-start | bytes 405512 | tf_op jit(solution)/shard_map/ppermute | solution.py:618
  71.0 8.3 %collective-permute-start.7 = (f32[264,128]{1,0:T(8,128)S(1)}, f32[264,128]{1,0:T(8,128)S(1)}, u32[]{:S(2)}, u32[]{:S(2)}) collective-permute-start(f32[264,128]{1,0:T(8,128)S(1)} %shard_map.108.n0), channel_id=1, source_target_pairs={{0,4},{1,5},{2,6},{3,7},{4,0},{5,1},{6,2},{7,3},{8,12},{9,13},{10,... | collective-permute-start | bytes 405512 | tf_op jit(solution)/shard_map/ppermute | solution.py:618
  71.7 7.5 %collective-permute-start.6 = (f32[264,128]{1,0:T(8,128)S(1)}, f32[264,128]{1,0:T(8,128)S(1)}, u32[]{:S(2)}, u32[]{:S(2)}) collective-permute-start(f32[264,128]{1,0:T(8,128)S(1)} %shard_map.108.n0), channel_id=1, source_target_pairs={{0,2},{1,3},{2,4},{3,5},{4,6},{5,7},{6,0},{7,1},{8,10},{9,11},{10,... | collective-permute-start | bytes 405512 | tf_op jit(solution)/shard_map/ppermute | solution.py:618
  79.3 23.3 %copy-start.10 = (s32[1,4,32]{2,1,0:T(4,128)S(1)}, s32[1,4,32]{2,1,0:T(4,128)}, u32[]{:S(2)}) copy-start(s32[1,4,32]{2,1,0:T(4,128)} %get-tuple-element.49.land) | copy-start | bytes 1540
  80.4 9.3 %collective-permute-start.9 = (f32[2,512,128]{2,1,0:T(8,128)S(1)}, f32[2,512,128]{2,1,0:T(8,128)S(1)}, u32[]{:S(2)}, u32[]{:S(2)}) collective-permute-start(f32[2,512,128]{2,1,0:T(8,128)S(1)} %get-tuple-element.71.own), channel_id=1, source_target_pairs={{0,1},{1,0},{2,3},{3,2},{4,5},{5,4},{6,7},{7,6},{8,9},{9,8},{10,11... | collective-permute-start | bytes 1572872 | tf_op jit(solution)/shard_map/ppermute | solution.py:615
  85.4 13.6 %all-to-all-start.2 = ((f32[32,5,2,128]{3,2,1,0:T(2,128)}), f32[32,5,2,128]{3,2,1,0:T(2,128)S(1)}, u32[]{:S(2)}, u32[]{:S(2)}) async-start(f32[32,5,2,128]{3,2,1,0:T(2,128)} %bitcast.8), calls=%async_computation.2 | async-start | bytes 327680 | tf_op jit(solution)/shard_map/all_to_all | solution.py:622
  99.0 3.6 %collective-permute-start.10 = (f32[320,128]{1,0:T(8,128)S(1)}, f32[320,128]{1,0:T(8,128)S(1)}, u32[]{:S(2)}, u32[]{:S(2)}) collective-permute-start(f32[320,128]{1,0:T(8,128)S(1)} %bitcast.20), channel_id=1, source_target_pairs={{0,1},{1,0},{2,3},{3,2},{4,5},{5,4},{6,7},{7,6},{8,9},{9,8},{10,11... | collective-permute-start | bytes 491528 | tf_op jit(solution)/shard_map/ppermute | solution.py:615
  108.7 1.5 collective-permute-start.11
  115.6 13.7 %collective-permute-start.12 = (f32[4,264,128]{2,1,0:T(8,128)S(1)}, f32[4,264,128]{2,1,0:T(8,128)S(1)}, u32[]{:S(2)}, u32[]{:S(2)}) collective-permute-start(f32[4,264,128]{2,1,0:T(8,128)S(1)} %get-tuple-element.82), channel_id=1, source_target_pairs={{0,1},{1,0},{2,3},{3,2},{4,5},{5,4},{6,7},{7,6},{8,9},{9,8},{10,11... | collective-permute-start | bytes 1622024 | tf_op jit(solution)/shard_map/ppermute | solution.py:615
  129.8 5.2 %collective-permute-start.13 = (f32[264,128]{1,0:T(8,128)S(1)}, f32[264,128]{1,0:T(8,128)S(1)}, u32[]{:S(2)}, u32[]{:S(2)}) collective-permute-start(f32[264,128]{1,0:T(8,128)S(1)} %get-tuple-element.84), channel_id=1, source_target_pairs={{0,2},{1,3},{2,4},{3,5},{4,6},{5,7},{6,0},{7,1},{8,10},{9,11},{10,... | collective-permute-start | bytes 405512 | tf_op jit(solution)/shard_map/ppermute | solution.py:618
  131.6 5.6 %collective-permute-start.14 = (f32[264,128]{1,0:T(8,128)S(1)}, f32[264,128]{1,0:T(8,128)S(1)}, u32[]{:S(2)}, u32[]{:S(2)}) collective-permute-start(f32[264,128]{1,0:T(8,128)S(1)} %get-tuple-element.85), channel_id=1, source_target_pairs={{0,4},{1,5},{2,6},{3,7},{4,0},{5,1},{6,2},{7,3},{8,12},{9,13},{10,... | collective-permute-start | bytes 405512 | tf_op jit(solution)/shard_map/ppermute | solution.py:618
  133.3 4.2 %collective-permute-start.15 = (f32[264,128]{1,0:T(8,128)S(1)}, f32[264,128]{1,0:T(8,128)S(1)}, u32[]{:S(2)}, u32[]{:S(2)}) collective-permute-start(f32[264,128]{1,0:T(8,128)S(1)} %get-tuple-element.86), channel_id=1, source_target_pairs={{0,6},{1,7},{2,0},{3,1},{4,2},{5,3},{6,4},{7,5},{8,14},{9,15},{10,... | collective-permute-start | bytes 405512 | tf_op jit(solution)/shard_map/ppermute | solution.py:618
  137.7 7.3 %collective-permute-start.18 = (f32[264,128]{1,0:T(8,128)S(1)}, f32[264,128]{1,0:T(8,128)S(1)}, u32[]{:S(2)}, u32[]{:S(2)}) collective-permute-start(f32[264,128]{1,0:T(8,128)S(1)} %shard_map.116.n0), channel_id=1, source_target_pairs={{0,6},{1,7},{2,0},{3,1},{4,2},{5,3},{6,4},{7,5},{8,14},{9,15},{10,... | collective-permute-start | bytes 405512 | tf_op jit(solution)/shard_map/ppermute | solution.py:618
  139.7 7.7 %collective-permute-start.17 = (f32[264,128]{1,0:T(8,128)S(1)}, f32[264,128]{1,0:T(8,128)S(1)}, u32[]{:S(2)}, u32[]{:S(2)}) collective-permute-start(f32[264,128]{1,0:T(8,128)S(1)} %shard_map.116.n0), channel_id=1, source_target_pairs={{0,4},{1,5},{2,6},{3,7},{4,0},{5,1},{6,2},{7,3},{8,12},{9,13},{10,... | collective-permute-start | bytes 405512 | tf_op jit(solution)/shard_map/ppermute | solution.py:618
  140.8 9.8 %collective-permute-start.16 = (f32[264,128]{1,0:T(8,128)S(1)}, f32[264,128]{1,0:T(8,128)S(1)}, u32[]{:S(2)}, u32[]{:S(2)}) collective-permute-start(f32[264,128]{1,0:T(8,128)S(1)} %shard_map.116.n0), channel_id=1, source_target_pairs={{0,2},{1,3},{2,4},{3,5},{4,6},{5,7},{6,0},{7,1},{8,10},{9,11},{10,... | collective-permute-start | bytes 405512 | tf_op jit(solution)/shard_map/ppermute | solution.py:618
  140.8 18.6 %collective-permute-start.19 = (f32[264,128]{1,0:T(8,128)S(1)}, f32[264,128]{1,0:T(8,128)S(1)}, u32[]{:S(2)}, u32[]{:S(2)}) collective-permute-start(f32[264,128]{1,0:T(8,128)S(1)} %shard_map.116.n0), channel_id=1, source_target_pairs={{0,1},{1,0},{2,3},{3,2},{4,5},{5,4},{6,7},{7,6},{8,9},{9,8},{10,11... | collective-permute-start | bytes 405512 | tf_op jit(solution)/shard_map/ppermute | solution.py:615
  145.0 14.5 %collective-permute-start.22 = (f32[264,128]{1,0:T(8,128)S(1)}, f32[264,128]{1,0:T(8,128)S(1)}, u32[]{:S(2)}, u32[]{:S(2)}) collective-permute-start(f32[264,128]{1,0:T(8,128)S(1)} %collective-permute-done.18.r3), channel_id=1, source_target_pairs={{0,1},{1,0},{2,3},{3,2},{4,5},{5,4},{6,7},{7,6},{8,9},{9,8},{10,11... | collective-permute-start | bytes 405512 | tf_op jit(solution)/shard_map/ppermute | solution.py:615
  147.4 12.1 %collective-permute-start.21 = (f32[264,128]{1,0:T(8,128)S(1)}, f32[264,128]{1,0:T(8,128)S(1)}, u32[]{:S(2)}, u32[]{:S(2)}) collective-permute-start(f32[264,128]{1,0:T(8,128)S(1)} %collective-permute-done.17.r2), channel_id=1, source_target_pairs={{0,1},{1,0},{2,3},{3,2},{4,5},{5,4},{6,7},{7,6},{8,9},{9,8},{10,11... | collective-permute-start | bytes 405512 | tf_op jit(solution)/shard_map/ppermute | solution.py:615
  150.6 8.9 %collective-permute-start.20 = (f32[264,128]{1,0:T(8,128)S(1)}, f32[264,128]{1,0:T(8,128)S(1)}, u32[]{:S(2)}, u32[]{:S(2)}) collective-permute-start(f32[264,128]{1,0:T(8,128)S(1)} %collective-permute-done.16.r1), channel_id=1, source_target_pairs={{0,1},{1,0},{2,3},{3,2},{4,5},{5,4},{6,7},{7,6},{8,9},{9,8},{10,11... | collective-permute-start | bytes 405512 | tf_op jit(solution)/shard_map/ppermute | solution.py:615

commit v2 on v1

--- a/solution.py
+++ b/solution.py
@@ -130,7 +130,7 @@
         colour[at, :] = colour[at, :] * live[k : k + 1]
     wide = jnp.concatenate([live, jnp.zeros((120, blends), F32)], axis=0).astype(BF16)
     ab = lax.dot_general(member, wide, NT, preferred_element_type=F32)
-    return live, ab, colour_table(member, colour[...])
+    return member, live, ab, colour_table(member, colour[...])
 
 
 def first_kernel(
@@ -158,7 +158,7 @@
     blocks = morph.shape[1]
     for c in arrivals[:3]:
         c.wait()
-    _, ab, table = begin(spectra, lengths, counts, colour, blocks)
+    _, _, ab, table = begin(spectra, lengths, counts, colour, blocks)
     for c in arrivals[3:]:
         c.wait()
     take = slots_by_block(sent[0], blocks)
@@ -216,8 +216,8 @@
     sent_far,
     land_far,
     observed_far,
-    own,
-    other,
+    own_far,
+    other_far,
     colour,
     alive,
     table,
@@ -227,6 +227,8 @@
     land,
     wide,
     resid_far,
+    own,
+    other,
     morph,
     spectra,
     counts,
@@ -235,6 +237,7 @@
     sems,
     sem_in,
     sem_out,
+    sem_pair,
 ):
     _, h = band_place()
     near = (lengths, counts, spectra, sent, land, morph)
@@ -249,7 +252,7 @@
     started([arrival(t) for t in tiles])
     for c in arrivals[:3]:
         c.wait()
-    live, ab, rows = begin(spectra, lengths, counts, colour, blocks)
+    member, live, ab, rows = begin(spectra, lengths, counts, colour, blocks)
     alive[...] = live
     ablk[...] = ab
     table[...] = rows
@@ -258,8 +261,16 @@
     for k2 in range(2):
         own[k2] = morph[k2 ^ (2 * h)] * ab[:, k2 : k2 + 1]
         other[k2] = morph[(k2 + 2) ^ (2 * h)] * ab[:, k2 + 2 : k2 + 3]
+    gone = started(
+        [
+            pltpu.make_async_copy(own, own_far, sem_pair.at[0]),
+            pltpu.make_async_copy(other, other_far, sem_pair.at[1]),
+        ]
+    )
+    wide[...] = powers(colour[...], member)
     model_loop(table, own, other, observed, resid, arrival, leaving)
-    wide[...] = powers(colour[...], membership_of(lengths[...], blocks))
+    for c in gone:
+        c.wait()
     for t in tiles:
         leaving(t).wait()
 
@@ -676,6 +687,8 @@
             observed,
         ),
         scratch=(
+            pltpu.VMEM(pair, F32),
+            pltpu.VMEM(pair, F32),
             pltpu.VMEM(morphology.shape, F32),
             pltpu.VMEM(spectra.shape, F32),
             pltpu.VMEM(counts.shape, jnp.int32),
@@ -684,11 +697,12 @@
             dma(6),
             dma(tiles),
             dma(tiles),
+            dma(2),
         ),
         cost=20e6,
         limit=67_043_328,
         far_in=range(7),
-        far_out=(10,),
+        far_out=(0, 1, 10),
     )
     for iteration in range(ITERS):
         last = iteration == ITERS - 1

time: 161 us -> 161 us (level)
  no operation moved by 1% of the time
where the time goes in v2:
time: 161 us
  Pallas kernels  59.8 us (37%)
  starting transfers between devices  54.9 us (34%)
  blocking collectives  29.5 us (18%)
  waiting for transfers between devices  14.8 us (9%)
    pallas_call x17, Pallas kernels, call(): pl.pallas_call(kernel, out_shape=shapes, in_specs=[far if i in far_in els...  59.8 us
    all_to_all x2, blocking collectives, over_tile(): return lax.all_to_all(v, 'tile', 0, 0, tiled=True).reshape(message)  29.5 us
    ppermute x11, starting transfers between devices, over_core(): return lax.ppermute(v, 'band', [(i, i ^ 1) for i in range(band)])  22.8 us
    all_to_all x2, starting transfers between devices, over_tile(): return lax.all_to_all(v, 'tile', 0, 0, tiled=True).reshape(message)  16.5 us
    ppermute x12, starting transfers between devices, over_x(): lax.ppermute(v, 'band', [(i, (i + 2 * step) % band) for i in range(band)])  15.6 us
    ppermute x12, waiting for transfers between devices, over_x(): lax.ppermute(v, 'band', [(i, (i + 2 * step) % band) for i in range(band)])  6.4 us
    ppermute x11, waiting for transfers between devices, over_core(): return lax.ppermute(v, 'band', [(i, i ^ 1) for i in range(band)])  4.34 us
    all_to_all x2, waiting for transfers between devices, over_tile(): return lax.all_to_all(v, 'tile', 0, 0, tiled=True).reshape(message)  4.02 us
  transfers between devices with their start and end apart: 25, of which 12 were waited for; matrix products, arithmetic and copies ran while one was open for 0% of the time, Pallas kernels for 18%

profile of v2, /device:TPU:1, one launch (start us, length us, event | category | flops | bytes accessed | tf_op | source)
XLA Modules:
  0.0 160.6 jit_solution(10494814766659078141)
XLA Ops:
  0.6 2.7 %shard_map.103 = f32[320,128]{1,0:T(8,128)} custom-call(f32[4,512,128]{2,1,0:T(8,128)} %morph_far.3, f32[12,4,256]{2,1,0:T(4,128)} %bitcast.23, s32[1,256]{1,0:T(1,128)} %lengths_far.3, s32[1,256]{1,0:T(1,128)} %bitcast.28, s32[1,4,32]{2,1,0:T(4,128)} %bitcast.26), custom_call_target="tpu_custom_call" | custom-call | bytes 3000000 | tf_op jit(solution)/shard_map/pallas_call | solution.py:597
  3.4 12.2 %all-to-all-start = ((f32[32,5,2,128]{3,2,1,0:T(2,128)}), f32[32,5,2,128]{3,2,1,0:T(2,128)}, u32[]{:S(2)}, u32[]{:S(2)}) async-start(f32[32,5,2,128]{3,2,1,0:T(2,128)} %bitcast.22), calls=%async_computation | async-start | bytes 327680 | tf_op jit(solution)/shard_map/all_to_all | solution.py:633
  15.5 8.4 %shard_map.104 = (f32[2,512,128]{2,1,0:T(8,128)}, f32[2,512,128]{2,1,0:T(8,128)}, f32[64,256]{1,0:T(8,128)}, f32[8,256]{1,0:T(8,128)}, f32[512,128]{1,0:T(8,128)...) custom-call(f32[4,512,128]{2,1,0:T(8,128)} %morph_far.3, ...), custom_call_target="tpu_custom_call" | custom-call | bytes 20000000 | tf_op jit(solution)/shard_map/pallas_call | solution.py:597
  24.0 0.9 all-to-all-done
  24.9 2.4 %collective-permute-start = (f32[320,128]{1,0:T(8,128)}, f32[320,128]{1,0:T(8,128)S(1)}, u32[]{:S(2)}, u32[]{:S(2)}) collective-permute-start(f32[320,128]{1,0:T(8,128)} %bitcast.4.mine), channel_id=1, source_target_pairs={{0,1},{1,0},{2,3},{3,2},{4,5},{5,4},{6,7},{7,6},{8,9},{9,8},{10,11... | collective-permute-start | bytes 491528 | tf_op jit(solution)/shard_map/ppermute | solution.py:626
  27.3 1.2 collective-permute-done.partner
  28.5 0.7 copy-done.9
  29.2 7.1 %shard_map.105 = (f32[12,512,128]{2,1,0:T(8,128)}, f32[320,128]{1,0:T(8,128)S(1)}, f32[320,128]{1,0:T(8,128)S(1)}, f32[8,512]{1,0:T(8,128)S(1)}) custom-call(f32[320,128]{1,0:T(8,128)} %bitcast.4.mine, f32[320,128]{1,0:T(8,128)S(1)} %collective-permute-done.partner, f32[12,512,128]{2,1,0:T(8,128)} %get-tuple-element.48.resid_far, ...), custom_call_target="tpu_custom_call" | custom-call | bytes 14000000 | tf_op jit(solution)/shard_map/pallas_call | solution.py:597
  36.7 1.0 collective-permute-done.1
  37.8 5.5 %shard_map.106 = (f32[4,264,128]{2,1,0:T(8,128)S(1)}, f32[4,264,128]{2,1,0:T(8,128)S(1)}) custom-call(f32[512,128]{1,0:T(8,128)S(1)} %copy-done.3, f32[12,512,128]{2,1,0:T(8,128)} %get-tuple-element.53.wgt_far, f32[8,512]{1,0:T(8,128)S(1)} %copy-done.7, f32[8,512]{1,0:T(8,128)S(1)} %get-tuple-element.55.miss, f32[320,128]{1,0:T(8,128)S(1)} %add.6.after), custom_call_target="tpu_custom_call" | custom-call | bytes 16000000 | tf_op jit(solution)/shard_map/pallas_call | solution.py:597
  43.7 16.2 %all_to_all.20 = f32[32,5,2,128]{3,2,1,0:T(2,128)S(1)} all-to-all(f32[32,5,2,128]{3,2,1,0:T(2,128)S(1)} %bitcast.15), channel_id=1, replica_groups=mesh['tile'=32,'band'=8] {'tile'}, dimensions={0} | all-to-all | bytes 327680 | tf_op jit(solution)/shard_map/all_to_all | solution.py:633
  60.0 0.5 shard_map.107
  60.5 1.3 collective-permute-start.3
  61.8 2.5 %collective-permute-start.4 = (f32[264,128]{1,0:T(8,128)S(1)}, f32[264,128]{1,0:T(8,128)S(1)}, u32[]{:S(2)}, u32[]{:S(2)}) collective-permute-start(f32[264,128]{1,0:T(8,128)S(1)} %get-tuple-element.61), channel_id=1, source_target_pairs={{0,4},{1,5},{2,6},{3,7},{4,0},{5,1},{6,2},{7,3},{8,12},{9,13},{10,... | collective-permute-start | bytes 405512 | tf_op jit(solution)/shard_map/ppermute | solution.py:629
  64.3 1.2 collective-permute-start.5
  65.7 2.5 %collective-permute-done.4.r2 = f32[264,128]{1,0:T(8,128)S(1)} collective-permute-done((f32[264,128]{1,0:T(8,128)S(1)}, f32[264,128]{1,0:T(8,128)S(1)}, u32[]{:S(2)}, u32[]{:S(2)}) %collective-permute-start.4) | collective-permute-done | bytes 135200 | tf_op jit(solution)/shard_map/ppermute | solution.py:629
  68.6 2.1 %collective-permute-start.8 = (f32[264,128]{1,0:T(8,128)S(1)}, f32[264,128]{1,0:T(8,128)S(1)}, u32[]{:S(2)}, u32[]{:S(2)}) collective-permute-start(f32[264,128]{1,0:T(8,128)S(1)} %shard_map.108.n0), channel_id=1, source_target_pairs={{0,6},{1,7},{2,0},{3,1},{4,2},{5,3},{6,4},{7,5},{8,14},{9,15},{10,... | collective-permute-start | bytes 405512 | tf_op jit(solution)/shard_map/ppermute | solution.py:629
  70.8 0.8 collective-permute-start.7
  71.9 4.7 %shard_map.109.per_block = f32[512,128]{1,0:T(8,128)S(1)} custom-call(f32[2,512,128]{2,1,0:T(8,128)S(1)} %copy-done, f32[2,512,128]{2,1,0:T(8,128)S(1)} %copy-done.1, f32[12,512,128]{2,1,0:T(8,128)} %get-tuple-element.53.wgt_far), custom_call_target="tpu_custom_call" | custom-call | bytes 16000000 | tf_op jit(solution)/shard_map/pallas_call | solution.py:597
  76.7 2.4 %shard_map.110 = (f32[64,256]{1,0:T(8,128)S(1)}, f32[512,128]{1,0:T(8,128)S(1)}) custom-call(f32[320,128]{1,0:T(8,128)S(1)} %bitcast.19, s32[1,4,32]{2,1,0:T(4,128)S(1)} %copy-done.5, f32[512,128]{1,0:T(8,128)S(1)} %shard_map.109.per_block, s32[1,256]{1,0:T(1,128)S(1)} %copy-done.8, f32[2,512,128]{2,1,0:T(8,128)S(1)} %copy-done, ...), custom_call_target="tpu_custom_call" | custom-call | bytes 8000000 | tf_op jit(solution)/shard_map/pallas_call | solution.py:597
  79.1 1.1 shard_map.111
  80.2 4.9 %collective-permute-start.9 = (f32[2,512,128]{2,1,0:T(8,128)S(1)}, f32[2,512,128]{2,1,0:T(8,128)S(1)}, u32[]{:S(2)}, u32[]{:S(2)}) collective-permute-start(f32[2,512,128]{2,1,0:T(8,128)S(1)} %get-tuple-element.71.own), channel_id=1, source_target_pairs={{0,1},{1,0},{2,3},{3,2},{4,5},{5,4},{6,7},{7,6},{8,9},{9,8},{10,11... | collective-permute-start | bytes 1572872 | tf_op jit(solution)/shard_map/ppermute | solution.py:626
  85.1 4.3 %all-to-all-start.2 = ((f32[32,5,2,128]{3,2,1,0:T(2,128)}), f32[32,5,2,128]{3,2,1,0:T(2,128)S(1)}, u32[]{:S(2)}, u32[]{:S(2)}) async-start(f32[32,5,2,128]{3,2,1,0:T(2,128)} %bitcast.8), calls=%async_computation.2 | async-start | bytes 327680 | tf_op jit(solution)/shard_map/all_to_all | solution.py:633
  89.5 6.1 %shard_map.112 = (f32[8,512]{1,0:T(8,128)S(1)}, f32[12,512,128]{2,1,0:T(8,128)}) custom-call(f32[512,128]{1,0:T(8,128)S(1)} %get-tuple-element.69.table, f32[2,512,128]{2,1,0:T(8,128)S(1)} %get-tuple-element.71.own, f32[2,512,128]{2,1,0:T(8,128)S(1)} %collective-permute-done.9.other, f32[64,256]{1,0:T(8,128)S(1)} %get-tuple-element.72.colour, ...), custom_call_target="tpu_custom_call" | custom-call | bytes 16000000 | tf_op jit(solution)/shard_map/pallas_call | solution.py:597
  95.6 3.1 %all-to-all-done.2 = f32[32,5,2,128]{3,2,1,0:T(2,128)S(1)} async-done(((f32[32,5,2,128]{3,2,1,0:T(2,128)}), f32[32,5,2,128]{3,2,1,0:T(2,128)S(1)}, u32[]{:S(2)}, u32[]{:S(2)}) %all-to-all-start.2) | async-done | bytes 163872 | tf_op jit(solution)/shard_map/all_to_all | solution.py:633
  98.7 2.6 %collective-permute-start.10 = (f32[320,128]{1,0:T(8,128)S(1)}, f32[320,128]{1,0:T(8,128)S(1)}, u32[]{:S(2)}, u32[]{:S(2)}) collective-permute-start(f32[320,128]{1,0:T(8,128)S(1)} %bitcast.20), channel_id=1, source_target_pairs={{0,1},{1,0},{2,3},{3,2},{4,5},{5,4},{6,7},{7,6},{8,9},{9,8},{10,11... | collective-permute-start | bytes 491528 | tf_op jit(solution)/shard_map/ppermute | solution.py:626
  101.3 1.0 collective-permute-done.10.partner
  102.4 6.1 %shard_map.113 = (f32[12,512,128]{2,1,0:T(8,128)}, f32[320,128]{1,0:T(8,128)S(1)}, f32[320,128]{1,0:T(8,128)S(1)}, f32[8,512]{1,0:T(8,128)S(1)}) custom-call(f32[320,128]{1,0:T(8,128)S(1)} %bitcast.21, f32[320,128]{1,0:T(8,128)S(1)} %collective-permute-done.10.partner, f32[12,512,128]{2,1,0:T(8,128)} %get-tuple-element.75.resid_far, ...), custom_call_target="tpu_custom_call" | custom-call | bytes 14000000 | tf_op jit(solution)/shard_map/pallas_call | solution.py:597
  108.5 0.5 collective-permute-start.11
  108.9 1.0 collective-permute-done.11
  110.0 5.4 %shard_map.114 = (f32[4,264,128]{2,1,0:T(8,128)S(1)}, f32[4,264,128]{2,1,0:T(8,128)S(1)}) custom-call(f32[512,128]{1,0:T(8,128)S(1)} %get-tuple-element.69.table, f32[12,512,128]{2,1,0:T(8,128)} %get-tuple-element.78.wgt_far, f32[8,512]{1,0:T(8,128)S(1)} %get-tuple-element.79.wide, f32[8,512]{1,0:T(8,128)S(1)} %get-tuple-element.80.miss, ...), custom_call_target="tpu_custom_call" | custom-call | bytes 16000000 | tf_op jit(solution)/shard_map/pallas_call | solution.py:597
  115.4 0.5 collective-permute-start.12
  115.9 13.2 %all_to_all.21 = f32[32,5,2,128]{3,2,1,0:T(2,128)S(1)} all-to-all(f32[32,5,2,128]{3,2,1,0:T(2,128)S(1)} %bitcast.14), channel_id=1, replica_groups=mesh['tile'=32,'band'=8] {'tile'}, dimensions={0} | all-to-all | bytes 327680 | tf_op jit(solution)/shard_map/all_to_all | solution.py:633
  129.1 0.5 shard_map.115
  129.6 1.8 %collective-permute-start.13 = (f32[264,128]{1,0:T(8,128)S(1)}, f32[264,128]{1,0:T(8,128)S(1)}, u32[]{:S(2)}, u32[]{:S(2)}) collective-permute-start(f32[264,128]{1,0:T(8,128)S(1)} %get-tuple-element.84), channel_id=1, source_target_pairs={{0,2},{1,3},{2,4},{3,5},{4,6},{5,7},{6,0},{7,1},{8,10},{9,11},{10,... | collective-permute-start | bytes 405512 | tf_op jit(solution)/shard_map/ppermute | solution.py:629
  131.4 1.7 %collective-permute-start.14 = (f32[264,128]{1,0:T(8,128)S(1)}, f32[264,128]{1,0:T(8,128)S(1)}, u32[]{:S(2)}, u32[]{:S(2)}) collective-permute-start(f32[264,128]{1,0:T(8,128)S(1)} %get-tuple-element.85), channel_id=1, source_target_pairs={{0,4},{1,5},{2,6},{3,7},{4,0},{5,1},{6,2},{7,3},{8,12},{9,13},{10,... | collective-permute-start | bytes 405512 | tf_op jit(solution)/shard_map/ppermute | solution.py:629
  133.1 0.8 collective-permute-start.15
  133.9 0.9 collective-permute-done.13.r1
  134.7 2.2 %collective-permute-done.14.r2 = f32[264,128]{1,0:T(8,128)S(1)} collective-permute-done((f32[264,128]{1,0:T(8,128)S(1)}, f32[264,128]{1,0:T(8,128)S(1)}, u32[]{:S(2)}, u32[]{:S(2)}) %collective-permute-start.14) | collective-permute-done | bytes 135200 | tf_op jit(solution)/shard_map/ppermute | solution.py:629
  137.4 2.0 %collective-permute-start.18 = (f32[264,128]{1,0:T(8,128)S(1)}, f32[264,128]{1,0:T(8,128)S(1)}, u32[]{:S(2)}, u32[]{:S(2)}) collective-permute-start(f32[264,128]{1,0:T(8,128)S(1)} %shard_map.116.n0), channel_id=1, source_target_pairs={{0,6},{1,7},{2,0},{3,1},{4,2},{5,3},{6,4},{7,5},{8,14},{9,15},{10,... | collective-permute-start | bytes 405512 | tf_op jit(solution)/shard_map/ppermute | solution.py:629
  139.4 1.2 collective-permute-start.17
  140.6 4.2 %collective-permute-start.19 = (f32[264,128]{1,0:T(8,128)S(1)}, f32[264,128]{1,0:T(8,128)S(1)}, u32[]{:S(2)}, u32[]{:S(2)}) collective-permute-start(f32[264,128]{1,0:T(8,128)S(1)} %shard_map.116.n0), channel_id=1, source_target_pairs={{0,1},{1,0},{2,3},{3,2},{4,5},{5,4},{6,7},{7,6},{8,9},{9,8},{10,11... | collective-permute-start | bytes 405512 | tf_op jit(solution)/shard_map/ppermute | solution.py:626
  144.8 2.4 %collective-permute-start.22 = (f32[264,128]{1,0:T(8,128)S(1)}, f32[264,128]{1,0:T(8,128)S(1)}, u32[]{:S(2)}, u32[]{:S(2)}) collective-permute-start(f32[264,128]{1,0:T(8,128)S(1)} %collective-permute-done.18.r3), channel_id=1, source_target_pairs={{0,1},{1,0},{2,3},{3,2},{4,5},{5,4},{6,7},{7,6},{8,9},{9,8},{10,11... | collective-permute-start | bytes 405512 | tf_op jit(solution)/shard_map/ppermute | solution.py:626
  147.2 3.1 %collective-permute-start.21 = (f32[264,128]{1,0:T(8,128)S(1)}, f32[264,128]{1,0:T(8,128)S(1)}, u32[]{:S(2)}, u32[]{:S(2)}) collective-permute-start(f32[264,128]{1,0:T(8,128)S(1)} %collective-permute-done.17.r2), channel_id=1, source_target_pairs={{0,1},{1,0},{2,3},{3,2},{4,5},{5,4},{6,7},{7,6},{8,9},{9,8},{10,11... | collective-permute-start | bytes 405512 | tf_op jit(solution)/shard_map/ppermute | solution.py:626
  150.3 1.4 collective-permute-start.20
  151.7 4.7 %shard_map.118.per_block = f32[512,128]{1,0:T(8,128)S(1)} custom-call(f32[2,512,128]{2,1,0:T(8,128)S(1)} %get-tuple-element.71.own, f32[2,512,128]{2,1,0:T(8,128)S(1)} %collective-permute-done.9.other, f32[12,512,128]{2,1,0:T(8,128)} %get-tuple-element.78.wgt_far), custom_call_target="tpu_custom_call" | custom-call | bytes 16000000 | tf_op jit(solution)/shard_map/pallas_call | solution.py:597
  156.4 2.8 %shard_map.119 = f32[12,4,256]{2,1,0:T(4,128)} custom-call(f32[320,128]{1,0:T(8,128)S(1)} %bitcast.17, s32[1,4,32]{2,1,0:T(4,128)S(1)} %copy-done.5, f32[512,128]{1,0:T(8,128)S(1)} %shard_map.118.per_block, s32[1,256]{1,0:T(1,128)S(1)} %copy-done.8, f32[2,512,128]{2,1,0:T(8,128)S(1)} %get-tuple-element.71.own, ...), custom_call_target="tpu_custom_call" | custom-call | bytes 8000000 | tf_op jit(solution)/shard_map/pallas_call | solution.py:597
  159.2 1.3 shard_map.117
  (45 shorter events, 2.6 us)
Async XLA Ops:
  3.4 21.5 %all-to-all-start = ((f32[32,5,2,128]{3,2,1,0:T(2,128)}), f32[32,5,2,128]{3,2,1,0:T(2,128)}, u32[]{:S(2)}, u32[]{:S(2)}) async-start(f32[32,5,2,128]{3,2,1,0:T(2,128)} %bitcast.22), calls=%async_computation | async-start | bytes 327680 | tf_op jit(solution)/shard_map/all_to_all | solution.py:633
  24.9 3.6 %collective-permute-start = (f32[320,128]{1,0:T(8,128)}, f32[320,128]{1,0:T(8,128)S(1)}, u32[]{:S(2)}, u32[]{:S(2)}) collective-permute-start(f32[320,128]{1,0:T(8,128)} %bitcast.4.mine), channel_id=1, source_target_pairs={{0,1},{1,0},{2,3},{3,2},{4,5},{5,4},{6,7},{7,6},{8,9},{9,8},{10,11... | collective-permute-start | bytes 491528 | tf_op jit(solution)/shard_map/ppermute | solution.py:626
  28.5 0.7 copy-start.9
  29.2 8.6 %copy-start.3 = (f32[512,128]{1,0:T(8,128)S(1)}, f32[512,128]{1,0:T(8,128)}, u32[]{:S(2)}) copy-start(f32[512,128]{1,0:T(8,128)} %get-tuple-element.52.table) | copy-start | bytes 786436
  29.2 8.6 %copy-start.7 = (f32[8,512]{1,0:T(8,128)S(1)}, f32[8,512]{1,0:T(8,128)}, u32[]{:S(2)}) copy-start(f32[8,512]{1,0:T(8,128)} %get-tuple-element.54.wide) | copy-start | bytes 49156
  36.2 23.7 %copy-start.5 = (s32[1,4,32]{2,1,0:T(4,128)S(1)}, s32[1,4,32]{2,1,0:T(4,128)}, u32[]{:S(2)}) copy-start(s32[1,4,32]{2,1,0:T(4,128)} %get-tuple-element.58.sent) | copy-start | bytes 1540
  36.3 32.2 %copy-start = (f32[2,512,128]{2,1,0:T(8,128)S(1)}, f32[2,512,128]{2,1,0:T(8,128)}, u32[]{:S(2)}) copy-start(f32[2,512,128]{2,1,0:T(8,128)} %get-tuple-element.63.own) | copy-start | bytes 1572868
  36.3 32.2 %copy-start.2 = (f32[512,128]{1,0:T(8,128)S(1)}, f32[512,128]{1,0:T(8,128)}, u32[]{:S(2)}) copy-start(f32[512,128]{1,0:T(8,128)} %get-tuple-element.64.ablk) | copy-start | bytes 786436
  36.3 1.5 collective-permute-start.1
  37.8 34.1 %copy-start.1 = (f32[2,512,128]{2,1,0:T(8,128)S(1)}, f32[2,512,128]{2,1,0:T(8,128)}, u32[]{:S(2)}) copy-start(f32[2,512,128]{2,1,0:T(8,128)} %get-tuple-element.65.other) | copy-start | bytes 1572868
  43.3 16.7 %collective-permute-start.2 = (f32[4,264,128]{2,1,0:T(8,128)S(1)}, f32[4,264,128]{2,1,0:T(8,128)S(1)}, u32[]{:S(2)}, u32[]{:S(2)}) collective-permute-start(f32[4,264,128]{2,1,0:T(8,128)S(1)} %get-tuple-element.57), channel_id=1, source_target_pairs={{0,1},{1,0},{2,3},{3,2},{4,5},{5,4},{6,7},{7,6},{8,9},{9,8},{10,11... | collective-permute-start | bytes 1622024 | tf_op jit(solution)/shard_map/ppermute | solution.py:626
  60.5 16.2 %copy-start.4 = (f32[64,256]{1,0:T(8,128)S(1)}, f32[64,256]{1,0:T(8,128)}, u32[]{:S(2)}) copy-start(f32[64,256]{1,0:T(8,128)} %get-tuple-element.67.colour) | copy-start | bytes 196612
  60.5 16.2 %copy-start.6 = (f32[8,256]{1,0:T(8,128)S(1)}, f32[8,256]{1,0:T(8,128)}, u32[]{:S(2)}) copy-start(f32[8,256]{1,0:T(8,128)} %get-tuple-element.68.alive) | copy-start | bytes 24580
  60.5 16.2 %copy-start.8 = (s32[1,256]{1,0:T(1,128)S(1)}, s32[1,256]{1,0:T(1,128)}, u32[]{:S(2)}) copy-start(s32[1,256]{1,0:T(1,128)} %get-tuple-element.66.lengths) | copy-start | bytes 3076
  60.5 5.2 %collective-permute-start.3 = (f32[264,128]{1,0:T(8,128)S(1)}, f32[264,128]{1,0:T(8,128)S(1)}, u32[]{:S(2)}, u32[]{:S(2)}) collective-permute-start(f32[264,128]{1,0:T(8,128)S(1)} %get-tuple-element.60), channel_id=1, source_target_pairs={{0,2},{1,3},{2,4},{3,5},{4,6},{5,7},{6,0},{7,1},{8,10},{9,11},{10,... | collective-permute-start | bytes 405512 | tf_op jit(solution)/shard_map/ppermute | solution.py:629
  61.8 6.4 %collective-permute-start.4 = (f32[264,128]{1,0:T(8,128)S(1)}, f32[264,128]{1,0:T(8,128)S(1)}, u32[]{:S(2)}, u32[]{:S(2)}) collective-permute-start(f32[264,128]{1,0:T(8,128)S(1)} %get-tuple-element.61), channel_id=1, source_target_pairs={{0,4},{1,5},{2,6},{3,7},{4,0},{5,1},{6,2},{7,3},{8,12},{9,13},{10,... | collective-permute-start | bytes 405512 | tf_op jit(solution)/shard_map/ppermute | solution.py:629
  64.3 4.2 %collective-permute-start.5 = (f32[264,128]{1,0:T(8,128)S(1)}, f32[264,128]{1,0:T(8,128)S(1)}, u32[]{:S(2)}, u32[]{:S(2)}) collective-permute-start(f32[264,128]{1,0:T(8,128)S(1)} %get-tuple-element.62), channel_id=1, source_target_pairs={{0,6},{1,7},{2,0},{3,1},{4,2},{5,3},{6,4},{7,5},{8,14},{9,15},{10,... | collective-permute-start | bytes 405512 | tf_op jit(solution)/shard_map/ppermute | solution.py:629
  68.6 10.4 %collective-permute-start.8 = (f32[264,128]{1,0:T(8,128)S(1)}, f32[264,128]{1,0:T(8,128)S(1)}, u32[]{:S(2)}, u32[]{:S(2)}) collective-permute-start(f32[264,128]{1,0:T(8,128)S(1)} %shard_map.108.n0), channel_id=1, source_target_pairs={{0,6},{1,7},{2,0},{3,1},{4,2},{5,3},{6,4},{7,5},{8,14},{9,15},{10,... | collective-permute-start | bytes 405512 | tf_op jit(solution)/shard_map/ppermute | solution.py:629
  70.8 8.3 %collective-permute-start.7 = (f32[264,128]{1,0:T(8,128)S(1)}, f32[264,128]{1,0:T(8,128)S(1)}, u32[]{:S(2)}, u32[]{:S(2)}) collective-permute-start(f32[264,128]{1,0:T(8,128)S(1)} %shard_map.108.n0), channel_id=1, source_target_pairs={{0,4},{1,5},{2,6},{3,7},{4,0},{5,1},{6,2},{7,3},{8,12},{9,13},{10,... | collective-permute-start | bytes 405512 | tf_op jit(solution)/shard_map/ppermute | solution.py:629
  71.5 7.6 %collective-permute-start.6 = (f32[264,128]{1,0:T(8,128)S(1)}, f32[264,128]{1,0:T(8,128)S(1)}, u32[]{:S(2)}, u32[]{:S(2)}) collective-permute-start(f32[264,128]{1,0:T(8,128)S(1)} %shard_map.108.n0), channel_id=1, source_target_pairs={{0,2},{1,3},{2,4},{3,5},{4,6},{5,7},{6,0},{7,1},{8,10},{9,11},{10,... | collective-permute-start | bytes 405512 | tf_op jit(solution)/shard_map/ppermute | solution.py:629
  79.1 23.3 %copy-start.10 = (s32[1,4,32]{2,1,0:T(4,128)S(1)}, s32[1,4,32]{2,1,0:T(4,128)}, u32[]{:S(2)}) copy-start(s32[1,4,32]{2,1,0:T(4,128)} %get-tuple-element.49.land) | copy-start | bytes 1540
  80.2 9.2 %collective-permute-start.9 = (f32[2,512,128]{2,1,0:T(8,128)S(1)}, f32[2,512,128]{2,1,0:T(8,128)S(1)}, u32[]{:S(2)}, u32[]{:S(2)}) collective-permute-start(f32[2,512,128]{2,1,0:T(8,128)S(1)} %get-tuple-element.71.own), channel_id=1, source_target_pairs={{0,1},{1,0},{2,3},{3,2},{4,5},{5,4},{6,7},{7,6},{8,9},{9,8},{10,11... | collective-permute-start | bytes 1572872 | tf_op jit(solution)/shard_map/ppermute | solution.py:626
  85.1 13.6 %all-to-all-start.2 = ((f32[32,5,2,128]{3,2,1,0:T(2,128)}), f32[32,5,2,128]{3,2,1,0:T(2,128)S(1)}, u32[]{:S(2)}, u32[]{:S(2)}) async-start(f32[32,5,2,128]{3,2,1,0:T(2,128)} %bitcast.8), calls=%async_computation.2 | async-start | bytes 327680 | tf_op jit(solution)/shard_map/all_to_all | solution.py:633
  98.7 3.6 %collective-permute-start.10 = (f32[320,128]{1,0:T(8,128)S(1)}, f32[320,128]{1,0:T(8,128)S(1)}, u32[]{:S(2)}, u32[]{:S(2)}) collective-permute-start(f32[320,128]{1,0:T(8,128)S(1)} %bitcast.20), channel_id=1, source_target_pairs={{0,1},{1,0},{2,3},{3,2},{4,5},{5,4},{6,7},{7,6},{8,9},{9,8},{10,11... | collective-permute-start | bytes 491528 | tf_op jit(solution)/shard_map/ppermute | solution.py:626
  108.5 1.5 collective-permute-start.11
  115.4 13.7 %collective-permute-start.12 = (f32[4,264,128]{2,1,0:T(8,128)S(1)}, f32[4,264,128]{2,1,0:T(8,128)S(1)}, u32[]{:S(2)}, u32[]{:S(2)}) collective-permute-start(f32[4,264,128]{2,1,0:T(8,128)S(1)} %get-tuple-element.82), channel_id=1, source_target_pairs={{0,1},{1,0},{2,3},{3,2},{4,5},{5,4},{6,7},{7,6},{8,9},{9,8},{10,11... | collective-permute-start | bytes 1622024 | tf_op jit(solution)/shard_map/ppermute | solution.py:626
  129.6 5.2 %collective-permute-start.13 = (f32[264,128]{1,0:T(8,128)S(1)}, f32[264,128]{1,0:T(8,128)S(1)}, u32[]{:S(2)}, u32[]{:S(2)}) collective-permute-start(f32[264,128]{1,0:T(8,128)S(1)} %get-tuple-element.84), channel_id=1, source_target_pairs={{0,2},{1,3},{2,4},{3,5},{4,6},{5,7},{6,0},{7,1},{8,10},{9,11},{10,... | collective-permute-start | bytes 405512 | tf_op jit(solution)/shard_map/ppermute | solution.py:629
  131.4 5.6 %collective-permute-start.14 = (f32[264,128]{1,0:T(8,128)S(1)}, f32[264,128]{1,0:T(8,128)S(1)}, u32[]{:S(2)}, u32[]{:S(2)}) collective-permute-start(f32[264,128]{1,0:T(8,128)S(1)} %get-tuple-element.85), channel_id=1, source_target_pairs={{0,4},{1,5},{2,6},{3,7},{4,0},{5,1},{6,2},{7,3},{8,12},{9,13},{10,... | collective-permute-start | bytes 405512 | tf_op jit(solution)/shard_map/ppermute | solution.py:629
  133.1 4.2 %collective-permute-start.15 = (f32[264,128]{1,0:T(8,128)S(1)}, f32[264,128]{1,0:T(8,128)S(1)}, u32[]{:S(2)}, u32[]{:S(2)}) collective-permute-start(f32[264,128]{1,0:T(8,128)S(1)} %get-tuple-element.86), channel_id=1, source_target_pairs={{0,6},{1,7},{2,0},{3,1},{4,2},{5,3},{6,4},{7,5},{8,14},{9,15},{10,... | collective-permute-start | bytes 405512 | tf_op jit(solution)/shard_map/ppermute | solution.py:629
  137.4 7.3 %collective-permute-start.18 = (f32[264,128]{1,0:T(8,128)S(1)}, f32[264,128]{1,0:T(8,128)S(1)}, u32[]{:S(2)}, u32[]{:S(2)}) collective-permute-start(f32[264,128]{1,0:T(8,128)S(1)} %shard_map.116.n0), channel_id=1, source_target_pairs={{0,6},{1,7},{2,0},{3,1},{4,2},{5,3},{6,4},{7,5},{8,14},{9,15},{10,... | collective-permute-start | bytes 405512 | tf_op jit(solution)/shard_map/ppermute | solution.py:629
  139.4 7.8 %collective-permute-start.17 = (f32[264,128]{1,0:T(8,128)S(1)}, f32[264,128]{1,0:T(8,128)S(1)}, u32[]{:S(2)}, u32[]{:S(2)}) collective-permute-start(f32[264,128]{1,0:T(8,128)S(1)} %shard_map.116.n0), channel_id=1, source_target_pairs={{0,4},{1,5},{2,6},{3,7},{4,0},{5,1},{6,2},{7,3},{8,12},{9,13},{10,... | collective-permute-start | bytes 405512 | tf_op jit(solution)/shard_map/ppermute | solution.py:629
  140.6 9.7 %collective-permute-start.16 = (f32[264,128]{1,0:T(8,128)S(1)}, f32[264,128]{1,0:T(8,128)S(1)}, u32[]{:S(2)}, u32[]{:S(2)}) collective-permute-start(f32[264,128]{1,0:T(8,128)S(1)} %shard_map.116.n0), channel_id=1, source_target_pairs={{0,2},{1,3},{2,4},{3,5},{4,6},{5,7},{6,0},{7,1},{8,10},{9,11},{10,... | collective-permute-start | bytes 405512 | tf_op jit(solution)/shard_map/ppermute | solution.py:629
  140.6 18.6 %collective-permute-start.19 = (f32[264,128]{1,0:T(8,128)S(1)}, f32[264,128]{1,0:T(8,128)S(1)}, u32[]{:S(2)}, u32[]{:S(2)}) collective-permute-start(f32[264,128]{1,0:T(8,128)S(1)} %shard_map.116.n0), channel_id=1, source_target_pairs={{0,1},{1,0},{2,3},{3,2},{4,5},{5,4},{6,7},{7,6},{8,9},{9,8},{10,11... | collective-permute-start | bytes 405512 | tf_op jit(solution)/shard_map/ppermute | solution.py:626
  144.8 14.5 %collective-permute-start.22 = (f32[264,128]{1,0:T(8,128)S(1)}, f32[264,128]{1,0:T(8,128)S(1)}, u32[]{:S(2)}, u32[]{:S(2)}) collective-permute-start(f32[264,128]{1,0:T(8,128)S(1)} %collective-permute-done.18.r3), channel_id=1, source_target_pairs={{0,1},{1,0},{2,3},{3,2},{4,5},{5,4},{6,7},{7,6},{8,9},{9,8},{10,11... | collective-permute-start | bytes 405512 | tf_op jit(solution)/shard_map/ppermute | solution.py:626
  147.2 12.0 %collective-permute-start.21 = (f32[264,128]{1,0:T(8,128)S(1)}, f32[264,128]{1,0:T(8,128)S(1)}, u32[]{:S(2)}, u32[]{:S(2)}) collective-permute-start(f32[264,128]{1,0:T(8,128)S(1)} %collective-permute-done.17.r2), channel_id=1, source_target_pairs={{0,1},{1,0},{2,3},{3,2},{4,5},{5,4},{6,7},{7,6},{8,9},{9,8},{10,11... | collective-permute-start | bytes 405512 | tf_op jit(solution)/shard_map/ppermute | solution.py:626
  150.3 8.9 %collective-permute-start.20 = (f32[264,128]{1,0:T(8,128)S(1)}, f32[264,128]{1,0:T(8,128)S(1)}, u32[]{:S(2)}, u32[]{:S(2)}) collective-permute-start(f32[264,128]{1,0:T(8,128)S(1)} %collective-permute-done.16.r1), channel_id=1, source_target_pairs={{0,1},{1,0},{2,3},{3,2},{4,5},{5,4},{6,7},{7,6},{8,9},{9,8},{10,11... | collective-permute-start | bytes 405512 | tf_op jit(solution)/shard_map/ppermute | solution.py:626

commit v3 on v2

--- a/solution.py
+++ b/solution.py
@@ -216,8 +216,19 @@
     sent_far,
     land_far,
     observed_far,
-    own_far,
-    other_far,
+    own_out,
+    other_out,
+    colour_out,
+    alive_out,
+    table_out,
+    ablk_out,
+    lengths_out,
+    sent_out,
+    land_out,
+    wide_out,
+    resid_far,
+    own,
+    other,
     colour,
     alive,
     table,
@@ -226,9 +237,6 @@
     sent,
     land,
     wide,
-    resid_far,
-    own,
-    other,
     morph,
     spectra,
     counts,
@@ -237,7 +245,7 @@
     sems,
     sem_in,
     sem_out,
-    sem_pair,
+    sem_state,
 ):
     _, h = band_place()
     near = (lengths, counts, spectra, sent, land, morph)
@@ -261,13 +269,23 @@
     for k2 in range(2):
         own[k2] = morph[k2 ^ (2 * h)] * ab[:, k2 : k2 + 1]
         other[k2] = morph[(k2 + 2) ^ (2 * h)] * ab[:, k2 + 2 : k2 + 3]
+    wide[...] = powers(colour[...], member)
+    state = (own, other, colour, alive, table, ablk, lengths, sent, land, wide)
+    outs = (
+        own_out,
+        other_out,
+        colour_out,
+        alive_out,
+        table_out,
+        ablk_out,
+        lengths_out,
+        sent_out,
+        land_out,
+        wide_out,
+    )
     gone = started(
-        [
-            pltpu.make_async_copy(own, own_far, sem_pair.at[0]),
-            pltpu.make_async_copy(other, other_far, sem_pair.at[1]),
-        ]
-    )
-    wide[...] = powers(colour[...], member)
+        [pltpu.make_async_copy(v, o, sem_state.at[i]) for i, (v, o) in enumerate(zip(state, outs))]
+    )
     model_loop(table, own, other, observed, resid, arrival, leaving)
     for c in gone:
         c.wait()
@@ -689,6 +707,14 @@
         scratch=(
             pltpu.VMEM(pair, F32),
             pltpu.VMEM(pair, F32),
+            pltpu.VMEM(colour_rows, F32),
+            pltpu.VMEM((8, blends), F32),
+            pltpu.VMEM(table_rows, F32),
+            pltpu.VMEM(table_rows, F32),
+            pltpu.VMEM(blend_blocks.shape, jnp.int32),
+            pltpu.VMEM(sent_blocks.shape, jnp.int32),
+            pltpu.VMEM(landing_blocks.shape, jnp.int32),
+            pltpu.VMEM((8, blocks), F32),
             pltpu.VMEM(morphology.shape, F32),
             pltpu.VMEM(spectra.shape, F32),
             pltpu.VMEM(counts.shape, jnp.int32),
@@ -697,12 +723,12 @@
             dma(6),
             dma(tiles),
             dma(tiles),
-            dma(2),
+            dma(10),
         ),
         cost=20e6,
         limit=67_043_328,
         far_in=range(7),
-        far_out=(0, 1, 10),
+        far_out=range(11),
     )
     for iteration in range(ITERS):
         last = iteration == ITERS - 1

time: 161 us -> 160 us (level)
  no operation moved by 1% of the time
where the time goes in v3:
time: 160 us
  Pallas kernels  58.8 us (37%)
  starting transfers between devices  54.9 us (34%)
  blocking collectives  28.5 us (18%)
  waiting for transfers between devices  15.8 us (10%)
    pallas_call x17, Pallas kernels, call(): pl.pallas_call(kernel, out_shape=shapes, in_specs=[far if i in far_in els...  58.8 us
    all_to_all x2, blocking collectives, over_tile(): return lax.all_to_all(v, 'tile', 0, 0, tiled=True).reshape(message)  28.5 us
    ppermute x11, starting transfers between devices, over_core(): return lax.ppermute(v, 'band', [(i, i ^ 1) for i in range(band)])  22.8 us
    all_to_all x2, starting transfers between devices, over_tile(): return lax.all_to_all(v, 'tile', 0, 0, tiled=True).reshape(message)  16.5 us
    ppermute x12, starting transfers between devices, over_x(): lax.ppermute(v, 'band', [(i, (i + 2 * step) % band) for i in range(band)])  15.6 us
    ppermute x12, waiting for transfers between devices, over_x(): lax.ppermute(v, 'band', [(i, (i + 2 * step) % band) for i in range(band)])  6.38 us
    all_to_all x2, waiting for transfers between devices, over_tile(): return lax.all_to_all(v, 'tile', 0, 0, tiled=True).reshape(message)  5.03 us
    ppermute x11, waiting for transfers between devices, over_core(): return lax.ppermute(v, 'band', [(i, i ^ 1) for i in range(band)])  4.34 us
  transfers between devices with their start and end apart: 25, of which 12 were waited for; matrix products, arithmetic and copies ran while one was open for 0% of the time, Pallas kernels for 18%

profile of v3, /device:TPU:1, one launch (start us, length us, event | category | flops | bytes accessed | tf_op | source)
XLA Modules:
  0.0 159.6 jit_solution(10355820560636090705)
XLA Ops:
  0.6 2.7 %shard_map.103 = f32[320,128]{1,0:T(8,128)} custom-call(f32[4,512,128]{2,1,0:T(8,128)} %morph_far.3, f32[12,4,256]{2,1,0:T(4,128)} %bitcast.23, s32[1,256]{1,0:T(1,128)} %lengths_far.3, s32[1,256]{1,0:T(1,128)} %bitcast.28, s32[1,4,32]{2,1,0:T(4,128)} %bitcast.26), custom_call_target="tpu_custom_call" | custom-call | bytes 3000000 | tf_op jit(solution)/shard_map/pallas_call | solution.py:615
  3.4 12.2 %all-to-all-start = ((f32[32,5,2,128]{3,2,1,0:T(2,128)}), f32[32,5,2,128]{3,2,1,0:T(2,128)}, u32[]{:S(2)}, u32[]{:S(2)}) async-start(f32[32,5,2,128]{3,2,1,0:T(2,128)} %bitcast.22), calls=%async_computation | async-start | bytes 327680 | tf_op jit(solution)/shard_map/all_to_all | solution.py:651
  15.5 7.4 %shard_map.104 = (f32[2,512,128]{2,1,0:T(8,128)}, f32[2,512,128]{2,1,0:T(8,128)}, f32[64,256]{1,0:T(8,128)}, f32[8,256]{1,0:T(8,128)}, f32[512,128]{1,0:T(8,128)...) custom-call(f32[4,512,128]{2,1,0:T(8,128)} %morph_far.3, ...), custom_call_target="tpu_custom_call" | custom-call | bytes 20000000 | tf_op jit(solution)/shard_map/pallas_call | solution.py:615
  23.0 1.9 %all-to-all-done = f32[32,5,2,128]{3,2,1,0:T(2,128)} async-done(((f32[32,5,2,128]{3,2,1,0:T(2,128)}), f32[32,5,2,128]{3,2,1,0:T(2,128)}, u32[]{:S(2)}, u32[]{:S(2)}) %all-to-all-start) | async-done | bytes 163872 | tf_op jit(solution)/shard_map/all_to_all | solution.py:651
  24.9 2.4 %collective-permute-start = (f32[320,128]{1,0:T(8,128)}, f32[320,128]{1,0:T(8,128)S(1)}, u32[]{:S(2)}, u32[]{:S(2)}) collective-permute-start(f32[320,128]{1,0:T(8,128)} %bitcast.4.mine), channel_id=1, source_target_pairs={{0,1},{1,0},{2,3},{3,2},{4,5},{5,4},{6,7},{7,6},{8,9},{9,8},{10,11... | collective-permute-start | bytes 491528 | tf_op jit(solution)/shard_map/ppermute | solution.py:644
  27.3 1.2 collective-permute-done.partner
  28.5 0.7 copy-done.9
  29.2 7.1 %shard_map.105 = (f32[12,512,128]{2,1,0:T(8,128)}, f32[320,128]{1,0:T(8,128)S(1)}, f32[320,128]{1,0:T(8,128)S(1)}, f32[8,512]{1,0:T(8,128)S(1)}) custom-call(f32[320,128]{1,0:T(8,128)} %bitcast.4.mine, f32[320,128]{1,0:T(8,128)S(1)} %collective-permute-done.partner, f32[12,512,128]{2,1,0:T(8,128)} %get-tuple-element.48.resid_far, ...), custom_call_target="tpu_custom_call" | custom-call | bytes 14000000 | tf_op jit(solution)/shard_map/pallas_call | solution.py:615
  36.7 1.0 collective-permute-done.1
  37.8 5.5 %shard_map.106 = (f32[4,264,128]{2,1,0:T(8,128)S(1)}, f32[4,264,128]{2,1,0:T(8,128)S(1)}) custom-call(f32[512,128]{1,0:T(8,128)S(1)} %copy-done.3, f32[12,512,128]{2,1,0:T(8,128)} %get-tuple-element.53.wgt_far, f32[8,512]{1,0:T(8,128)S(1)} %copy-done.7, f32[8,512]{1,0:T(8,128)S(1)} %get-tuple-element.55.miss, f32[320,128]{1,0:T(8,128)S(1)} %add.6.after), custom_call_target="tpu_custom_call" | custom-call | bytes 16000000 | tf_op jit(solution)/shard_map/pallas_call | solution.py:615
  43.7 15.2 %all_to_all.20 = f32[32,5,2,128]{3,2,1,0:T(2,128)S(1)} all-to-all(f32[32,5,2,128]{3,2,1,0:T(2,128)S(1)} %bitcast.15), channel_id=1, replica_groups=mesh['tile'=32,'band'=8] {'tile'}, dimensions={0} | all-to-all | bytes 327680 | tf_op jit(solution)/shard_map/all_to_all | solution.py:651
  59.0 0.5 shard_map.107
  59.5 1.3 collective-permute-start.3
  60.8 2.4 %collective-permute-start.4 = (f32[264,128]{1,0:T(8,128)S(1)}, f32[264,128]{1,0:T(8,128)S(1)}, u32[]{:S(2)}, u32[]{:S(2)}) collective-permute-start(f32[264,128]{1,0:T(8,128)S(1)} %get-tuple-element.61), channel_id=1, source_target_pairs={{0,4},{1,5},{2,6},{3,7},{4,0},{5,1},{6,2},{7,3},{8,12},{9,13},{10,... | collective-permute-start | bytes 405512 | tf_op jit(solution)/shard_map/ppermute | solution.py:647
  63.2 1.2 collective-permute-start.5
  64.6 2.5 %collective-permute-done.4.r2 = f32[264,128]{1,0:T(8,128)S(1)} collective-permute-done((f32[264,128]{1,0:T(8,128)S(1)}, f32[264,128]{1,0:T(8,128)S(1)}, u32[]{:S(2)}, u32[]{:S(2)}) %collective-permute-start.4) | collective-permute-done | bytes 135200 | tf_op jit(solution)/shard_map/ppermute | solution.py:647
  67.6 2.2 %collective-permute-start.8 = (f32[264,128]{1,0:T(8,128)S(1)}, f32[264,128]{1,0:T(8,128)S(1)}, u32[]{:S(2)}, u32[]{:S(2)}) collective-permute-start(f32[264,128]{1,0:T(8,128)S(1)} %shard_map.108.n0), channel_id=1, source_target_pairs={{0,6},{1,7},{2,0},{3,1},{4,2},{5,3},{6,4},{7,5},{8,14},{9,15},{10,... | collective-permute-start | bytes 405512 | tf_op jit(solution)/shard_map/ppermute | solution.py:647
  69.8 0.8 collective-permute-start.7
  70.9 4.7 %shard_map.109.per_block = f32[512,128]{1,0:T(8,128)S(1)} custom-call(f32[2,512,128]{2,1,0:T(8,128)S(1)} %copy-done, f32[2,512,128]{2,1,0:T(8,128)S(1)} %copy-done.1, f32[12,512,128]{2,1,0:T(8,128)} %get-tuple-element.53.wgt_far), custom_call_target="tpu_custom_call" | custom-call | bytes 16000000 | tf_op jit(solution)/shard_map/pallas_call | solution.py:615
  75.7 2.4 %shard_map.110 = (f32[64,256]{1,0:T(8,128)S(1)}, f32[512,128]{1,0:T(8,128)S(1)}) custom-call(f32[320,128]{1,0:T(8,128)S(1)} %bitcast.19, s32[1,4,32]{2,1,0:T(4,128)S(1)} %copy-done.5, f32[512,128]{1,0:T(8,128)S(1)} %shard_map.109.per_block, s32[1,256]{1,0:T(1,128)S(1)} %copy-done.8, f32[2,512,128]{2,1,0:T(8,128)S(1)} %copy-done, ...), custom_call_target="tpu_custom_call" | custom-call | bytes 8000000 | tf_op jit(solution)/shard_map/pallas_call | solution.py:615
  78.1 1.1 shard_map.111
  79.2 4.9 %collective-permute-start.9 = (f32[2,512,128]{2,1,0:T(8,128)S(1)}, f32[2,512,128]{2,1,0:T(8,128)S(1)}, u32[]{:S(2)}, u32[]{:S(2)}) collective-permute-start(f32[2,512,128]{2,1,0:T(8,128)S(1)} %get-tuple-element.71.own), channel_id=1, source_target_pairs={{0,1},{1,0},{2,3},{3,2},{4,5},{5,4},{6,7},{7,6},{8,9},{9,8},{10,11... | collective-permute-start | bytes 1572872 | tf_op jit(solution)/shard_map/ppermute | solution.py:644
  84.1 4.3 %all-to-all-start.2 = ((f32[32,5,2,128]{3,2,1,0:T(2,128)}), f32[32,5,2,128]{3,2,1,0:T(2,128)S(1)}, u32[]{:S(2)}, u32[]{:S(2)}) async-start(f32[32,5,2,128]{3,2,1,0:T(2,128)} %bitcast.8), calls=%async_computation.2 | async-start | bytes 327680 | tf_op jit(solution)/shard_map/all_to_all | solution.py:651
  88.5 6.1 %shard_map.112 = (f32[8,512]{1,0:T(8,128)S(1)}, f32[12,512,128]{2,1,0:T(8,128)}) custom-call(f32[512,128]{1,0:T(8,128)S(1)} %get-tuple-element.69.table, f32[2,512,128]{2,1,0:T(8,128)S(1)} %get-tuple-element.71.own, f32[2,512,128]{2,1,0:T(8,128)S(1)} %collective-permute-done.9.other, f32[64,256]{1,0:T(8,128)S(1)} %get-tuple-element.72.colour, ...), custom_call_target="tpu_custom_call" | custom-call | bytes 16000000 | tf_op jit(solution)/shard_map/pallas_call | solution.py:615
  94.6 3.1 %all-to-all-done.2 = f32[32,5,2,128]{3,2,1,0:T(2,128)S(1)} async-done(((f32[32,5,2,128]{3,2,1,0:T(2,128)}), f32[32,5,2,128]{3,2,1,0:T(2,128)S(1)}, u32[]{:S(2)}, u32[]{:S(2)}) %all-to-all-start.2) | async-done | bytes 163872 | tf_op jit(solution)/shard_map/all_to_all | solution.py:651
  97.7 2.6 %collective-permute-start.10 = (f32[320,128]{1,0:T(8,128)S(1)}, f32[320,128]{1,0:T(8,128)S(1)}, u32[]{:S(2)}, u32[]{:S(2)}) collective-permute-start(f32[320,128]{1,0:T(8,128)S(1)} %bitcast.20), channel_id=1, source_target_pairs={{0,1},{1,0},{2,3},{3,2},{4,5},{5,4},{6,7},{7,6},{8,9},{9,8},{10,11... | collective-permute-start | bytes 491528 | tf_op jit(solution)/shard_map/ppermute | solution.py:644
  100.3 1.0 collective-permute-done.10.partner
  101.4 6.1 %shard_map.113 = (f32[12,512,128]{2,1,0:T(8,128)}, f32[320,128]{1,0:T(8,128)S(1)}, f32[320,128]{1,0:T(8,128)S(1)}, f32[8,512]{1,0:T(8,128)S(1)}) custom-call(f32[320,128]{1,0:T(8,128)S(1)} %bitcast.21, f32[320,128]{1,0:T(8,128)S(1)} %collective-permute-done.10.partner, f32[12,512,128]{2,1,0:T(8,128)} %get-tuple-element.75.resid_far, ...), custom_call_target="tpu_custom_call" | custom-call | bytes 14000000 | tf_op jit(solution)/shard_map/pallas_call | solution.py:615
  107.5 0.5 collective-permute-start.11
  107.9 1.0 collective-permute-done.11
  109.0 5.4 %shard_map.114 = (f32[4,264,128]{2,1,0:T(8,128)S(1)}, f32[4,264,128]{2,1,0:T(8,128)S(1)}) custom-call(f32[512,128]{1,0:T(8,128)S(1)} %get-tuple-element.69.table, f32[12,512,128]{2,1,0:T(8,128)} %get-tuple-element.78.wgt_far, f32[8,512]{1,0:T(8,128)S(1)} %get-tuple-element.79.wide, f32[8,512]{1,0:T(8,128)S(1)} %get-tuple-element.80.miss, ...), custom_call_target="tpu_custom_call" | custom-call | bytes 16000000 | tf_op jit(solution)/shard_map/pallas_call | solution.py:615
  114.4 0.5 collective-permute-start.12
  114.9 13.2 %all_to_all.21 = f32[32,5,2,128]{3,2,1,0:T(2,128)S(1)} all-to-all(f32[32,5,2,128]{3,2,1,0:T(2,128)S(1)} %bitcast.14), channel_id=1, replica_groups=mesh['tile'=32,'band'=8] {'tile'}, dimensions={0} | all-to-all | bytes 327680 | tf_op jit(solution)/shard_map/all_to_all | solution.py:651
  128.1 0.5 shard_map.115
  128.6 1.8 %collective-permute-start.13 = (f32[264,128]{1,0:T(8,128)S(1)}, f32[264,128]{1,0:T(8,128)S(1)}, u32[]{:S(2)}, u32[]{:S(2)}) collective-permute-start(f32[264,128]{1,0:T(8,128)S(1)} %get-tuple-element.84), channel_id=1, source_target_pairs={{0,2},{1,3},{2,4},{3,5},{4,6},{5,7},{6,0},{7,1},{8,10},{9,11},{10,... | collective-permute-start | bytes 405512 | tf_op jit(solution)/shard_map/ppermute | solution.py:647
  130.4 1.7 %collective-permute-start.14 = (f32[264,128]{1,0:T(8,128)S(1)}, f32[264,128]{1,0:T(8,128)S(1)}, u32[]{:S(2)}, u32[]{:S(2)}) collective-permute-start(f32[264,128]{1,0:T(8,128)S(1)} %get-tuple-element.85), channel_id=1, source_target_pairs={{0,4},{1,5},{2,6},{3,7},{4,0},{5,1},{6,2},{7,3},{8,12},{9,13},{10,... | collective-permute-start | bytes 405512 | tf_op jit(solution)/shard_map/ppermute | solution.py:647
  132.1 0.8 collective-permute-start.15
  132.9 0.9 collective-permute-done.13.r1
  133.7 2.2 %collective-permute-done.14.r2 = f32[264,128]{1,0:T(8,128)S(1)} collective-permute-done((f32[264,128]{1,0:T(8,128)S(1)}, f32[264,128]{1,0:T(8,128)S(1)}, u32[]{:S(2)}, u32[]{:S(2)}) %collective-permute-start.14) | collective-permute-done | bytes 135200 | tf_op jit(solution)/shard_map/ppermute | solution.py:647
  136.4 2.0 %collective-permute-start.18 = (f32[264,128]{1,0:T(8,128)S(1)}, f32[264,128]{1,0:T(8,128)S(1)}, u32[]{:S(2)}, u32[]{:S(2)}) collective-permute-start(f32[264,128]{1,0:T(8,128)S(1)} %shard_map.116.n0), channel_id=1, source_target_pairs={{0,6},{1,7},{2,0},{3,1},{4,2},{5,3},{6,4},{7,5},{8,14},{9,15},{10,... | collective-permute-start | bytes 405512 | tf_op jit(solution)/shard_map/ppermute | solution.py:647
  138.4 1.2 collective-permute-start.17
  139.6 4.1 %collective-permute-start.19 = (f32[264,128]{1,0:T(8,128)S(1)}, f32[264,128]{1,0:T(8,128)S(1)}, u32[]{:S(2)}, u32[]{:S(2)}) collective-permute-start(f32[264,128]{1,0:T(8,128)S(1)} %shard_map.116.n0), channel_id=1, source_target_pairs={{0,1},{1,0},{2,3},{3,2},{4,5},{5,4},{6,7},{7,6},{8,9},{9,8},{10,11... | collective-permute-start | bytes 405512 | tf_op jit(solution)/shard_map/ppermute | solution.py:644
  143.8 2.4 %collective-permute-start.22 = (f32[264,128]{1,0:T(8,128)S(1)}, f32[264,128]{1,0:T(8,128)S(1)}, u32[]{:S(2)}, u32[]{:S(2)}) collective-permute-start(f32[264,128]{1,0:T(8,128)S(1)} %collective-permute-done.18.r3), channel_id=1, source_target_pairs={{0,1},{1,0},{2,3},{3,2},{4,5},{5,4},{6,7},{7,6},{8,9},{9,8},{10,11... | collective-permute-start | bytes 405512 | tf_op jit(solution)/shard_map/ppermute | solution.py:644
  146.2 3.2 %collective-permute-start.21 = (f32[264,128]{1,0:T(8,128)S(1)}, f32[264,128]{1,0:T(8,128)S(1)}, u32[]{:S(2)}, u32[]{:S(2)}) collective-permute-start(f32[264,128]{1,0:T(8,128)S(1)} %collective-permute-done.17.r2), channel_id=1, source_target_pairs={{0,1},{1,0},{2,3},{3,2},{4,5},{5,4},{6,7},{7,6},{8,9},{9,8},{10,11... | collective-permute-start | bytes 405512 | tf_op jit(solution)/shard_map/ppermute | solution.py:644
  149.4 1.4 collective-permute-start.20
  150.7 4.7 %shard_map.118.per_block = f32[512,128]{1,0:T(8,128)S(1)} custom-call(f32[2,512,128]{2,1,0:T(8,128)S(1)} %get-tuple-element.71.own, f32[2,512,128]{2,1,0:T(8,128)S(1)} %collective-permute-done.9.other, f32[12,512,128]{2,1,0:T(8,128)} %get-tuple-element.78.wgt_far), custom_call_target="tpu_custom_call" | custom-call | bytes 16000000 | tf_op jit(solution)/shard_map/pallas_call | solution.py:615
  155.4 2.8 %shard_map.119 = f32[12,4,256]{2,1,0:T(4,128)} custom-call(f32[320,128]{1,0:T(8,128)S(1)} %bitcast.17, s32[1,4,32]{2,1,0:T(4,128)S(1)} %copy-done.5, f32[512,128]{1,0:T(8,128)S(1)} %shard_map.118.per_block, s32[1,256]{1,0:T(1,128)S(1)} %copy-done.8, f32[2,512,128]{2,1,0:T(8,128)S(1)} %get-tuple-element.71.own, ...), custom_call_target="tpu_custom_call" | custom-call | bytes 8000000 | tf_op jit(solution)/shard_map/pallas_call | solution.py:615
  158.3 1.3 shard_map.117
  (45 shorter events, 2.6 us)
Async XLA Ops:
  3.4 21.5 %all-to-all-start = ((f32[32,5,2,128]{3,2,1,0:T(2,128)}), f32[32,5,2,128]{3,2,1,0:T(2,128)}, u32[]{:S(2)}, u32[]{:S(2)}) async-start(f32[32,5,2,128]{3,2,1,0:T(2,128)} %bitcast.22), calls=%async_computation | async-start | bytes 327680 | tf_op jit(solution)/shard_map/all_to_all | solution.py:651
  24.9 3.6 %collective-permute-start = (f32[320,128]{1,0:T(8,128)}, f32[320,128]{1,0:T(8,128)S(1)}, u32[]{:S(2)}, u32[]{:S(2)}) collective-permute-start(f32[320,128]{1,0:T(8,128)} %bitcast.4.mine), channel_id=1, source_target_pairs={{0,1},{1,0},{2,3},{3,2},{4,5},{5,4},{6,7},{7,6},{8,9},{9,8},{10,11... | collective-permute-start | bytes 491528 | tf_op jit(solution)/shard_map/ppermute | solution.py:644
  28.5 0.7 copy-start.9
  29.2 8.6 %copy-start.3 = (f32[512,128]{1,0:T(8,128)S(1)}, f32[512,128]{1,0:T(8,128)}, u32[]{:S(2)}) copy-start(f32[512,128]{1,0:T(8,128)} %get-tuple-element.52.table) | copy-start | bytes 786436
  29.2 8.6 %copy-start.7 = (f32[8,512]{1,0:T(8,128)S(1)}, f32[8,512]{1,0:T(8,128)}, u32[]{:S(2)}) copy-start(f32[8,512]{1,0:T(8,128)} %get-tuple-element.54.wide) | copy-start | bytes 49156
  36.2 22.7 %copy-start.5 = (s32[1,4,32]{2,1,0:T(4,128)S(1)}, s32[1,4,32]{2,1,0:T(4,128)}, u32[]{:S(2)}) copy-start(s32[1,4,32]{2,1,0:T(4,128)} %get-tuple-element.58.sent) | copy-start | bytes 1540
  36.3 31.1 %copy-start = (f32[2,512,128]{2,1,0:T(8,128)S(1)}, f32[2,512,128]{2,1,0:T(8,128)}, u32[]{:S(2)}) copy-start(f32[2,512,128]{2,1,0:T(8,128)} %get-tuple-element.63.own) | copy-start | bytes 1572868
  36.3 31.1 %copy-start.2 = (f32[512,128]{1,0:T(8,128)S(1)}, f32[512,128]{1,0:T(8,128)}, u32[]{:S(2)}) copy-start(f32[512,128]{1,0:T(8,128)} %get-tuple-element.64.ablk) | copy-start | bytes 786436
  36.3 1.5 collective-permute-start.1
  37.8 33.1 %copy-start.1 = (f32[2,512,128]{2,1,0:T(8,128)S(1)}, f32[2,512,128]{2,1,0:T(8,128)}, u32[]{:S(2)}) copy-start(f32[2,512,128]{2,1,0:T(8,128)} %get-tuple-element.65.other) | copy-start | bytes 1572868
  43.3 15.7 %collective-permute-start.2 = (f32[4,264,128]{2,1,0:T(8,128)S(1)}, f32[4,264,128]{2,1,0:T(8,128)S(1)}, u32[]{:S(2)}, u32[]{:S(2)}) collective-permute-start(f32[4,264,128]{2,1,0:T(8,128)S(1)} %get-tuple-element.57), channel_id=1, source_target_pairs={{0,1},{1,0},{2,3},{3,2},{4,5},{5,4},{6,7},{7,6},{8,9},{9,8},{10,11... | collective-permute-start | bytes 1622024 | tf_op jit(solution)/shard_map/ppermute | solution.py:644
  59.5 16.2 %copy-start.4 = (f32[64,256]{1,0:T(8,128)S(1)}, f32[64,256]{1,0:T(8,128)}, u32[]{:S(2)}) copy-start(f32[64,256]{1,0:T(8,128)} %get-tuple-element.67.colour) | copy-start | bytes 196612
  59.5 16.2 %copy-start.6 = (f32[8,256]{1,0:T(8,128)S(1)}, f32[8,256]{1,0:T(8,128)}, u32[]{:S(2)}) copy-start(f32[8,256]{1,0:T(8,128)} %get-tuple-element.68.alive) | copy-start | bytes 24580
  59.5 16.2 %copy-start.8 = (s32[1,256]{1,0:T(1,128)S(1)}, s32[1,256]{1,0:T(1,128)}, u32[]{:S(2)}) copy-start(s32[1,256]{1,0:T(1,128)} %get-tuple-element.66.lengths) | copy-start | bytes 3076
  59.5 5.2 %collective-permute-start.3 = (f32[264,128]{1,0:T(8,128)S(1)}, f32[264,128]{1,0:T(8,128)S(1)}, u32[]{:S(2)}, u32[]{:S(2)}) collective-permute-start(f32[264,128]{1,0:T(8,128)S(1)} %get-tuple-element.60), channel_id=1, source_target_pairs={{0,2},{1,3},{2,4},{3,5},{4,6},{5,7},{6,0},{7,1},{8,10},{9,11},{10,... | collective-permute-start | bytes 405512 | tf_op jit(solution)/shard_map/ppermute | solution.py:647
  60.8 6.4 %collective-permute-start.4 = (f32[264,128]{1,0:T(8,128)S(1)}, f32[264,128]{1,0:T(8,128)S(1)}, u32[]{:S(2)}, u32[]{:S(2)}) collective-permute-start(f32[264,128]{1,0:T(8,128)S(1)} %get-tuple-element.61), channel_id=1, source_target_pairs={{0,4},{1,5},{2,6},{3,7},{4,0},{5,1},{6,2},{7,3},{8,12},{9,13},{10,... | collective-permute-start | bytes 405512 | tf_op jit(solution)/shard_map/ppermute | solution.py:647
  63.2 4.2 %collective-permute-start.5 = (f32[264,128]{1,0:T(8,128)S(1)}, f32[264,128]{1,0:T(8,128)S(1)}, u32[]{:S(2)}, u32[]{:S(2)}) collective-permute-start(f32[264,128]{1,0:T(8,128)S(1)} %get-tuple-element.62), channel_id=1, source_target_pairs={{0,6},{1,7},{2,0},{3,1},{4,2},{5,3},{6,4},{7,5},{8,14},{9,15},{10,... | collective-permute-start | bytes 405512 | tf_op jit(solution)/shard_map/ppermute | solution.py:647
  67.6 10.5 %collective-permute-start.8 = (f32[264,128]{1,0:T(8,128)S(1)}, f32[264,128]{1,0:T(8,128)S(1)}, u32[]{:S(2)}, u32[]{:S(2)}) collective-permute-start(f32[264,128]{1,0:T(8,128)S(1)} %shard_map.108.n0), channel_id=1, source_target_pairs={{0,6},{1,7},{2,0},{3,1},{4,2},{5,3},{6,4},{7,5},{8,14},{9,15},{10,... | collective-permute-start | bytes 405512 | tf_op jit(solution)/shard_map/ppermute | solution.py:647
  69.8 8.3 %collective-permute-start.7 = (f32[264,128]{1,0:T(8,128)S(1)}, f32[264,128]{1,0:T(8,128)S(1)}, u32[]{:S(2)}, u32[]{:S(2)}) collective-permute-start(f32[264,128]{1,0:T(8,128)S(1)} %shard_map.108.n0), channel_id=1, source_target_pairs={{0,4},{1,5},{2,6},{3,7},{4,0},{5,1},{6,2},{7,3},{8,12},{9,13},{10,... | collective-permute-start | bytes 405512 | tf_op jit(solution)/shard_map/ppermute | solution.py:647
  70.5 7.6 %collective-permute-start.6 = (f32[264,128]{1,0:T(8,128)S(1)}, f32[264,128]{1,0:T(8,128)S(1)}, u32[]{:S(2)}, u32[]{:S(2)}) collective-permute-start(f32[264,128]{1,0:T(8,128)S(1)} %shard_map.108.n0), channel_id=1, source_target_pairs={{0,2},{1,3},{2,4},{3,5},{4,6},{5,7},{6,0},{7,1},{8,10},{9,11},{10,... | collective-permute-start | bytes 405512 | tf_op jit(solution)/shard_map/ppermute | solution.py:647
  78.0 23.3 %copy-start.10 = (s32[1,4,32]{2,1,0:T(4,128)S(1)}, s32[1,4,32]{2,1,0:T(4,128)}, u32[]{:S(2)}) copy-start(s32[1,4,32]{2,1,0:T(4,128)} %get-tuple-element.49.land) | copy-start | bytes 1540
  79.2 9.3 %collective-permute-start.9 = (f32[2,512,128]{2,1,0:T(8,128)S(1)}, f32[2,512,128]{2,1,0:T(8,128)S(1)}, u32[]{:S(2)}, u32[]{:S(2)}) collective-permute-start(f32[2,512,128]{2,1,0:T(8,128)S(1)} %get-tuple-element.71.own), channel_id=1, source_target_pairs={{0,1},{1,0},{2,3},{3,2},{4,5},{5,4},{6,7},{7,6},{8,9},{9,8},{10,11... | collective-permute-start | bytes 1572872 | tf_op jit(solution)/shard_map/ppermute | solution.py:644
  84.1 13.6 %all-to-all-start.2 = ((f32[32,5,2,128]{3,2,1,0:T(2,128)}), f32[32,5,2,128]{3,2,1,0:T(2,128)S(1)}, u32[]{:S(2)}, u32[]{:S(2)}) async-start(f32[32,5,2,128]{3,2,1,0:T(2,128)} %bitcast.8), calls=%async_computation.2 | async-start | bytes 327680 | tf_op jit(solution)/shard_map/all_to_all | solution.py:651
  97.7 3.6 %collective-permute-start.10 = (f32[320,128]{1,0:T(8,128)S(1)}, f32[320,128]{1,0:T(8,128)S(1)}, u32[]{:S(2)}, u32[]{:S(2)}) collective-permute-start(f32[320,128]{1,0:T(8,128)S(1)} %bitcast.20), channel_id=1, source_target_pairs={{0,1},{1,0},{2,3},{3,2},{4,5},{5,4},{6,7},{7,6},{8,9},{9,8},{10,11... | collective-permute-start | bytes 491528 | tf_op jit(solution)/shard_map/ppermute | solution.py:644
  107.5 1.5 collective-permute-start.11
  114.4 13.7 %collective-permute-start.12 = (f32[4,264,128]{2,1,0:T(8,128)S(1)}, f32[4,264,128]{2,1,0:T(8,128)S(1)}, u32[]{:S(2)}, u32[]{:S(2)}) collective-permute-start(f32[4,264,128]{2,1,0:T(8,128)S(1)} %get-tuple-element.82), channel_id=1, source_target_pairs={{0,1},{1,0},{2,3},{3,2},{4,5},{5,4},{6,7},{7,6},{8,9},{9,8},{10,11... | collective-permute-start | bytes 1622024 | tf_op jit(solution)/shard_map/ppermute | solution.py:644
  128.6 5.2 %collective-permute-start.13 = (f32[264,128]{1,0:T(8,128)S(1)}, f32[264,128]{1,0:T(8,128)S(1)}, u32[]{:S(2)}, u32[]{:S(2)}) collective-permute-start(f32[264,128]{1,0:T(8,128)S(1)} %get-tuple-element.84), channel_id=1, source_target_pairs={{0,2},{1,3},{2,4},{3,5},{4,6},{5,7},{6,0},{7,1},{8,10},{9,11},{10,... | collective-permute-start | bytes 405512 | tf_op jit(solution)/shard_map/ppermute | solution.py:647
  130.4 5.6 %collective-permute-start.14 = (f32[264,128]{1,0:T(8,128)S(1)}, f32[264,128]{1,0:T(8,128)S(1)}, u32[]{:S(2)}, u32[]{:S(2)}) collective-permute-start(f32[264,128]{1,0:T(8,128)S(1)} %get-tuple-element.85), channel_id=1, source_target_pairs={{0,4},{1,5},{2,6},{3,7},{4,0},{5,1},{6,2},{7,3},{8,12},{9,13},{10,... | collective-permute-start | bytes 405512 | tf_op jit(solution)/shard_map/ppermute | solution.py:647
  132.1 4.2 %collective-permute-start.15 = (f32[264,128]{1,0:T(8,128)S(1)}, f32[264,128]{1,0:T(8,128)S(1)}, u32[]{:S(2)}, u32[]{:S(2)}) collective-permute-start(f32[264,128]{1,0:T(8,128)S(1)} %get-tuple-element.86), channel_id=1, source_target_pairs={{0,6},{1,7},{2,0},{3,1},{4,2},{5,3},{6,4},{7,5},{8,14},{9,15},{10,... | collective-permute-start | bytes 405512 | tf_op jit(solution)/shard_map/ppermute | solution.py:647
  136.4 7.3 %collective-permute-start.18 = (f32[264,128]{1,0:T(8,128)S(1)}, f32[264,128]{1,0:T(8,128)S(1)}, u32[]{:S(2)}, u32[]{:S(2)}) collective-permute-start(f32[264,128]{1,0:T(8,128)S(1)} %shard_map.116.n0), channel_id=1, source_target_pairs={{0,6},{1,7},{2,0},{3,1},{4,2},{5,3},{6,4},{7,5},{8,14},{9,15},{10,... | collective-permute-start | bytes 405512 | tf_op jit(solution)/shard_map/ppermute | solution.py:647
  138.4 7.7 %collective-permute-start.17 = (f32[264,128]{1,0:T(8,128)S(1)}, f32[264,128]{1,0:T(8,128)S(1)}, u32[]{:S(2)}, u32[]{:S(2)}) collective-permute-start(f32[264,128]{1,0:T(8,128)S(1)} %shard_map.116.n0), channel_id=1, source_target_pairs={{0,4},{1,5},{2,6},{3,7},{4,0},{5,1},{6,2},{7,3},{8,12},{9,13},{10,... | collective-permute-start | bytes 405512 | tf_op jit(solution)/shard_map/ppermute | solution.py:647
  139.6 9.8 %collective-permute-start.16 = (f32[264,128]{1,0:T(8,128)S(1)}, f32[264,128]{1,0:T(8,128)S(1)}, u32[]{:S(2)}, u32[]{:S(2)}) collective-permute-start(f32[264,128]{1,0:T(8,128)S(1)} %shard_map.116.n0), channel_id=1, source_target_pairs={{0,2},{1,3},{2,4},{3,5},{4,6},{5,7},{6,0},{7,1},{8,10},{9,11},{10,... | collective-permute-start | bytes 405512 | tf_op jit(solution)/shard_map/ppermute | solution.py:647
  139.6 18.6 %collective-permute-start.19 = (f32[264,128]{1,0:T(8,128)S(1)}, f32[264,128]{1,0:T(8,128)S(1)}, u32[]{:S(2)}, u32[]{:S(2)}) collective-permute-start(f32[264,128]{1,0:T(8,128)S(1)} %shard_map.116.n0), channel_id=1, source_target_pairs={{0,1},{1,0},{2,3},{3,2},{4,5},{5,4},{6,7},{7,6},{8,9},{9,8},{10,11... | collective-permute-start | bytes 405512 | tf_op jit(solution)/shard_map/ppermute | solution.py:644
  143.8 14.5 %collective-permute-start.22 = (f32[264,128]{1,0:T(8,128)S(1)}, f32[264,128]{1,0:T(8,128)S(1)}, u32[]{:S(2)}, u32[]{:S(2)}) collective-permute-start(f32[264,128]{1,0:T(8,128)S(1)} %collective-permute-done.18.r3), channel_id=1, source_target_pairs={{0,1},{1,0},{2,3},{3,2},{4,5},{5,4},{6,7},{7,6},{8,9},{9,8},{10,11... | collective-permute-start | bytes 405512 | tf_op jit(solution)/shard_map/ppermute | solution.py:644
  146.2 12.1 %collective-permute-start.21 = (f32[264,128]{1,0:T(8,128)S(1)}, f32[264,128]{1,0:T(8,128)S(1)}, u32[]{:S(2)}, u32[]{:S(2)}) collective-permute-start(f32[264,128]{1,0:T(8,128)S(1)} %collective-permute-done.17.r2), channel_id=1, source_target_pairs={{0,1},{1,0},{2,3},{3,2},{4,5},{5,4},{6,7},{7,6},{8,9},{9,8},{10,11... | collective-permute-start | bytes 405512 | tf_op jit(solution)/shard_map/ppermute | solution.py:644
  149.4 8.9 %collective-permute-start.20 = (f32[264,128]{1,0:T(8,128)S(1)}, f32[264,128]{1,0:T(8,128)S(1)}, u32[]{:S(2)}, u32[]{:S(2)}) collective-permute-start(f32[264,128]{1,0:T(8,128)S(1)} %collective-permute-done.16.r1), channel_id=1, source_target_pairs={{0,1},{1,0},{2,3},{3,2},{4,5},{5,4},{6,7},{7,6},{8,9},{9,8},{10,11... | collective-permute-start | bytes 405512 | tf_op jit(solution)/shard_map/ppermute | solution.py:644
